TPU v7x, 256 devices: a whole 4x4x8 slice. The times are simulated.
256 devices in a mesh: layer: 4 (over y), row: 4 (over x), col: 16 (over z, core).
Axes of the slice: x: 4, y: 4, z: 8, core: 2. Of those that a mesh axis runs over, the one named last changes fastest.
Arguments:
- root_rhs: bfloat16 [1024, 8192], P(('layer', 'col'), 'row'), may hold values from -6 to 6
- root_inverse: bfloat16 [8192, 8192], P('row', 'col'), may hold values from -0.0625 to 0.0625
- child_rhs: bfloat16 [4, 1024, 8192], P('layer', 'col', 'row'), may hold values from -6 to 6
- child_inverse: bfloat16 [4, 8192, 8192], P('layer', 'row', 'col'), may hold values from -0.0625 to 0.0625
- off_diagonal: bfloat16 [4, 8192, 8192], P('layer', 'col', 'row'), may hold values from -0.09375 to 0.09375
- pattern: int32 [4, 16, 16], P('layer'), may hold values 0 or 1
Outputs:
- root_solution: bfloat16 [1024, 8192], P(('layer', 'row'), 'col')
- child_solution: bfloat16 [4, 1024, 8192], P('layer', 'row', 'col')
All inputs are finite; a program needn't handle non-finite values. No bound on the sum of `pattern` on one device may be relied on, other than what follows from the above.
Results may differ from a plain program's by a relative error of at most 0.019.
Values may be sent and summed in bfloat16 or wider, within the bound.
No kernel may reach another device: no remote copies, remote signals or barrier semaphores. Data moves between devices by JAX's collectives and lax.ppermute only.
A program may use at most 64 MiB of HBM per device.

v0:
```python
import jax
import jax.numpy as jnp
from jax import lax
from jax.sharding import PartitionSpec as P

BR = 16
BC = 16


def on_device(root_rhs, root_inverse, child_rhs, child_inverse, off_diagonal, pattern):
    row_devices = lax.axis_size("row")
    col_devices = lax.axis_size("col")
    gathered = lax.all_gather(root_rhs, "col", axis=0, tiled=True)
    solved = lax.psum_scatter(
        jnp.dot(gathered, root_inverse, preferred_element_type=jnp.float32).astype(jnp.bfloat16),
        "row",
        scatter_dimension=0,
        tiled=True,
    )
    full_root = lax.all_gather(solved, ("layer", "row"), axis=0, tiled=True)
    mask_rows = BR // col_devices
    mask_cols = BC // row_devices
    local_pattern = lax.dynamic_slice(
        pattern[0],
        (lax.axis_index("col") * mask_rows, lax.axis_index("row") * mask_cols),
        (mask_rows, mask_cols),
    )
    height = off_diagonal.shape[1]
    breadth = off_diagonal.shape[2]
    masked = (
        off_diagonal[0].reshape(mask_rows, height // mask_rows, mask_cols, breadth // mask_cols)
        * local_pattern.astype(jnp.bfloat16)[:, None, :, None]
    ).reshape(height, breadth)
    whole_rhs = lax.all_gather(child_rhs[0], "col", axis=0, tiled=True)
    update = lax.psum(
        jnp.dot(full_root, masked, preferred_element_type=jnp.float32).astype(jnp.bfloat16), "col"
    ).astype(jnp.float32)
    reduced = (whole_rhs.astype(jnp.float32) - update).astype(jnp.bfloat16)
    child_solution = lax.psum_scatter(
        jnp.dot(reduced, child_inverse[0], preferred_element_type=jnp.float32).astype(jnp.bfloat16),
        "row",
        scatter_dimension=0,
        tiled=True,
    )
    return (solved, child_solution[None])


def solution(mesh):
    in_specs = (
        P(("layer", "col"), "row"),
        P("row", "col"),
        P("layer", "col", "row"),
        P("layer", "row", "col"),
        P("layer", "col", "row"),
        P("layer", None, None),
    )
    out_specs = (P(("layer", "row"), "col"), P("layer", "row", "col"))
    return jax.shard_map(
        on_device, mesh=mesh, in_specs=in_specs, out_specs=out_specs, check_vma=False
    )
```

profile of v0, /device:TPU:8, one launch (start us, length us, event | category | flops | bytes accessed | tf_op | source)
XLA Modules:
  0.0 336.8 jit_solution(9517561312611229891)
XLA Ops:
  7.2 0.0 copy-start
  7.2 0.0 all-gather.5.cloned.1.call-start
  7.2 0.7 all-gather.5.cloned.1.call-update
  7.9 0.0 reduce-scatter.3.cloned.1.call-start
  8.0 43.3 %all-gather.5.cloned.1.call-done = bf16[256,2048]{1,0:T(8,128)(2,1)} async-done(((bf16[16,2048]{1,0:T(8,128)(2,1)}), bf16[256,2048]{1,0:T(8,128)(2,1)}) %all-gather.5.cloned.1.call-update) | async-done | bytes 1048592 | tf_op jit(solution)/shard_map/all_gather | solution.py:13
  51.3 3.3 convolution_convert_fusion.1
  54.6 0.0 reduce-scatter.3.cloned.1.call-update
  54.6 0.0 all-gather.7.cloned.1.call-start
  54.7 22.0 %reduce-scatter.3.cloned.1.call-done = bf16[64,512]{1,0:T(8,128)(2,1)} async-done(((bf16[256,512]{1,0:T(8,128)(2,1)}), bf16[64,512]{1,0:T(8,128)(2,1)}) %reduce-scatter.3.cloned.1.call-update) | async-done | bytes 65552 | tf_op jit(solution)/shard_map/reduce_scatter | solution.py:14
  76.7 0.0 all-gather.7.cloned.1.call-update
  76.7 0.0 all-reduce.2.cloned.1.call-start
  76.8 0.8 convert_bitcast_fusion
  77.5 0.1 broadcast_bitcast_fusion
  77.6 49.0 %all-gather.7.cloned.1.call-done = bf16[1024,512]{1,0:T(8,128)(2,1)} async-done(((bf16[64,512]{1,0:T(8,128)(2,1)}), bf16[1024,512]{1,0:T(8,128)(2,1)}) %all-gather.7.cloned.1.call-update) | async-done | bytes 1048592 | tf_op jit(solution)/shard_map/all_gather | solution.py:20
  126.6 6.2 %convolution_convert_fusion = bf16[1024,2048]{1,0:T(8,128)(2,1)} fusion(bf16[1024,512]{1,0:T(8,128)(2,1)} %all-gather.7.cloned.1.call-done, bf16[1,512,2048]{2,1,0:T(8,128)(2,1)} %param.10, bf16[2048]{0:T(1024)(128)(2,1)S(1)} %bitcast.25), kind=kOutput, calls=%fused_computation.4 | convolution fusion | flops 2150629376 | bytes 7344128 | tf_op jit(solution)/shard_map/dot_general | solution.py:36
  132.9 0.0 all-reduce.2.cloned.1.call-update
  132.9 0.0 all-gather.9.cloned.1.call-start
  132.9 0.5 all-gather.9.cloned.1.call-update
  133.5 0.0 reduce-scatter.5.cloned.1.call-start
  133.5 121.0 %all-reduce.2.cloned.1.call-done = bf16[1024,2048]{1,0:T(8,128)(2,1)} async-done(((bf16[1024,2048]{1,0:T(8,128)(2,1)}), bf16[1024,2048]{1,0:T(8,128)(2,1)}) %all-reduce.2.cloned.1.call-update) | async-done | bytes 4194320 | tf_op jit(solution)/shard_map/psum | solution.py:35
  254.5 43.5 %all-gather.9.cloned.1.call-done = bf16[1,1024,2048]{2,1,0:T(8,128)(2,1)} async-done(((bf16[1,64,2048]{2,1,0:T(8,128)(2,1)}), bf16[1,1024,2048]{2,1,0:T(8,128)(2,1)}) %all-gather.9.cloned.1.call-update) | async-done | bytes 4194320 | tf_op jit(solution)/shard_map/all_gather | solution.py:34
  298.0 6.9 %fusion.5 = bf16[1024,512]{1,0:T(8,128)(2,1)} fusion(bf16[1,2048,512]{2,1,0:T(8,128)(2,1)S(1)} %copy-done, bf16[1024,2048]{1,0:T(8,128)(2,1)} %all-reduce.2.cloned.1.call-done, bf16[1,1024,2048]{2,1,0:T(8,128)(2,1)} %all-gather.9.cloned.1.call-done), kind=kOutput, calls=%fused_computation.7 | convolution fusion | flops 2156396544 | bytes 11534336 | tf_op jit(solution)/shard_map/dot_general | solution.py:40
  304.9 0.0 reduce-scatter.5.cloned.1.call-update
  304.9 25.0 %reduce-scatter.5.cloned.1.call-done = bf16[256,512]{1,0:T(8,128)(2,1)} async-done(((bf16[1024,512]{1,0:T(8,128)(2,1)}), bf16[256,512]{1,0:T(8,128)(2,1)}) %reduce-scatter.5.cloned.1.call-update) | async-done | bytes 262160 | tf_op jit(solution)/shard_map/reduce_scatter | solution.py:39
  (2 shorter events, 0.0 us)
Async XLA Ops:
  7.2 290.9 %copy-start = (bf16[1,2048,512]{2,1,0:T(8,128)(2,1)S(1)}, bf16[1,2048,512]{2,1,0:T(8,128)(2,1)}, u32[]{:S(2)}) copy-start(bf16[1,2048,512]{2,1,0:T(8,128)(2,1)} %param.9) | copy-start | bytes 6291460
  7.2 44.1 %all-gather.5.cloned.1.call-start = ((), (), s32[]{:S(2)}) async-start(), calls=%async_computation.2 | async-start | bytes 1114112 | tf_op jit(solution)/shard_map/all_gather | solution.py:13
  7.9 68.8 %reduce-scatter.3.cloned.1.call-start = ((), (), s32[]{:S(2)}) async-start(), calls=%async_computation.3 | async-start | bytes 327680 | tf_op jit(solution)/shard_map/reduce_scatter | solution.py:14
  54.6 72.0 %all-gather.7.cloned.1.call-start = ((), (), s32[]{:S(2)}) async-start(), calls=%async_computation.4 | async-start | bytes 1114112 | tf_op jit(solution)/shard_map/all_gather | solution.py:20
  76.7 177.8 %all-reduce.2.cloned.1.call-start = ((), (), s32[]{:S(2)}) async-start(), calls=%async_computation.5 | async-start | bytes 8388608 | tf_op jit(solution)/shard_map/psum | solution.py:35
  132.9 165.1 %all-gather.9.cloned.1.call-start = ((), (), s32[]{:S(2)}) async-start(), calls=%async_computation.7 | async-start | bytes 4456448 | tf_op jit(solution)/shard_map/all_gather | solution.py:34
  133.5 196.5 %reduce-scatter.5.cloned.1.call-start = ((), (), s32[]{:S(2)}) async-start(), calls=%async_computation.6 | async-start | bytes 1310720 | tf_op jit(solution)/shard_map/reduce_scatter | solution.py:39
Sparse Core Ops, SparseCore 0:
  9.8 41.4 all-gather.4
  54.8 21.8 reduce-scatter.2
  79.7 46.8 all-gather.6
  133.0 121.4 all-reduce.1
  256.2 41.7 all-gather.8
  305.0 24.8 reduce-scatter.4
where the time goes:
time: 337 us
  waiting for transfers between devices  305 us (91%)
  matrix products  16.4 us (5%)
  between operations  14.1 us (4%)
    psum x1, waiting for transfers between devices, on_device(): lax.psum(jnp.dot(full_root, masked, preferred_element_type=jnp.float32).a...  121 us
    all_gather x1, waiting for transfers between devices, on_device(): full_root = lax.all_gather(solved, ('layer', 'row'), axis=0, tiled=True)  49 us
    all_gather x1, waiting for transfers between devices, on_device(): whole_rhs = lax.all_gather(child_rhs[0], 'col', axis=0, tiled=True)  43.5 us
    all_gather x1, waiting for transfers between devices, on_device(): gathered = lax.all_gather(root_rhs, 'col', axis=0, tiled=True)  43.3 us
    reduce_scatter x1, waiting for transfers between devices, on_device(): lax.psum_scatter(jnp.dot(reduced, child_inverse[0], preferred_element_typ...  25 us
    reduce_scatter x1, waiting for transfers between devices, on_device(): lax.psum_scatter(jnp.dot(gathered, root_inverse, preferred_element_type=j...  22 us
    dot_general x1, matrix products, on_device(): jnp.dot(reduced, child_inverse[0], preferred_element_type=jnp.float32)  6.88 us
  transfers between devices with their start and end apart: 6, of which 6 were waited for; matrix products, arithmetic and copies ran while one was open for 0% of the time, Pallas kernels for 0%

commit v1 on v0

v1 whole, which is shorter than its diff:
```python
import jax
import jax.numpy as jnp
from jax import lax
from jax.experimental import pallas as pl
from jax.experimental.pallas import tpu as pltpu
from jax.sharding import PartitionSpec as P


BF = jnp.bfloat16
F32 = jnp.float32
NZ = 8
NX = 4
BC = 16
REACH = ((4, 3), (3, 4))


def to_core(x):
    return lax.ppermute(x, "col", [(i, i ^ 1) for i in range(2 * NZ)])


def twisted(x, step=1):
    pairs = []
    for i in range(2 * NZ):
        z, c = i // 2, i % 2
        pairs.append((i, 2 * ((z + (step if c == 0 else -step)) % NZ) + c))
    return lax.ppermute(x, "col", pairs)


def along_z(x, step):
    return lax.ppermute(x, "col", [(i, (i + 2 * step) % (2 * NZ)) for i in range(2 * NZ)])


def exchange(x, axes):
    return lax.all_to_all(x, axes, 0, 0, tiled=True)


def pick(x, index):
    return lax.dynamic_index_in_dim(x, index, 0, keepdims=False)


def put(x, piece, index):
    return lax.dynamic_update_index_in_dim(x, piece, index, 0)


def dot(a, b):
    return jnp.dot(a, b, preferred_element_type=F32)


def root_kernel(at, home, one, two, three, four, f12, f34, a, out, x):
    z, c = at[0], at[1]
    sign = 1 - 2 * c
    n = home.shape[0]
    h = n // 2

    def place(value, chip, core):
        start = pl.multiple_of((chip & (NZ - 1)) * n + core * h, h)
        x[pl.ds(start, h), :] = value

    def pair(ref, start, chip, core):
        place(ref[start : start + h, :], chip, core)
        place(ref[start + h : start + n, :], chip, 1 - core)

    pair(home, 0, z, c)
    pair(one, 0, z - sign, c)
    pair(two, 0, z - 2 * sign, c)
    pair(three, 0, z - 3 * sign, c)
    place(four[...], z + 4, c)
    pair(f12, 0, z + sign, 1 - c)
    pair(f12, n, z + 2 * sign, 1 - c)
    pair(f34, 0, z + 3 * sign, 1 - c)
    place(f34[n:, :], z + 4, 1 - c)
    out[...] = dot(x[...], a[...]).astype(BF)


def child_product(c, near, far, inverse):
    depth = near.shape[1]
    own_rows = pl.ds(pl.multiple_of(c * depth, depth), depth)
    far_rows = pl.ds(pl.multiple_of((1 - c) * depth, depth), depth)
    return (dot(near[...], inverse[own_rows, :]) + dot(far[...], inverse[far_rows, :])).astype(BF)


def first_kernel(at, near, far, inverse, out):
    out[...] = child_product(at[1], near, far, inverse)


def second_kernel(at, near, far, inverse, before, out):
    block = child_product(at[1], near, far, inverse)
    n = before.shape[0] // NZ
    for i in range(NZ):
        out[2 * i * n : (2 * i + 1) * n, :] = before[i * n : (i + 1) * n, :]
        out[(2 * i + 1) * n : (2 * i + 2) * n, :] = block[i * n : (i + 1) * n, :]


def local_call(kernel, rows, width, inputs, flops, scratch=()):
    vmem = pl.BlockSpec(memory_space=pltpu.VMEM)
    size = sum(x.size * x.dtype.itemsize for x in inputs)
    return pl.pallas_call(
        kernel,
        out_shape=jax.ShapeDtypeStruct((rows, width), BF),
        in_specs=[pl.BlockSpec(memory_space=pltpu.SMEM)] + [vmem] * (len(inputs) - 1),
        out_specs=vmem,
        scratch_shapes=scratch,
        compiler_params=pltpu.CompilerParams(vmem_limit_bytes=16 * 2**20),
        cost_estimate=pl.CostEstimate(
            flops=flops, bytes_accessed=size + 2 * rows * width, transcendentals=0
        ),
    )(*inputs)


def on_device(root_rhs, root_inverse, child_rhs, child_inverse, off_diagonal, pattern):
    r = lax.axis_index("row")
    k = lax.axis_index("col")
    z = k >> 1
    c = k & 1
    first = c == 0

    height, breadth = off_diagonal.shape[1:]
    half = breadth // 2
    blocks = BC // NX
    rows = child_rhs.shape[1]
    width = child_inverse.shape[2]
    small, depth = root_rhs.shape

    other = to_core(root_rhs)
    home = jnp.concatenate([root_rhs, other])
    four = twisted(home[:small], 4)
    three = twisted(home, 3)
    two = twisted(home, 2)
    one = twisted(home, 1)
    couple_own = lax.dynamic_slice(off_diagonal[0], (0, c * half), (height, half))
    couple_out = lax.dynamic_slice(off_diagonal[0], (0, (1 - c) * half), (height, half))
    rhs_own = lax.dynamic_slice(child_rhs[0], (0, c * half), (rows, half))
    rhs_out = lax.dynamic_slice(child_rhs[0], (0, (1 - c) * half), (rows, half))
    f43 = to_core(jnp.concatenate([three, four]))
    f12 = to_core(jnp.concatenate([one, two]))
    couple_far, rhs_far = to_core(couple_out), to_core(rhs_out)
    f12, couple_far, rhs_far, couple_own = lax.optimization_barrier(
        (f12, couple_far, rhs_far, couple_own)
    )
    rhs = (jnp.where(first, rhs_own, rhs_far), jnp.where(first, rhs_far, rhs_own))
    masks = lax.dynamic_slice(pattern[0], (2 * z, r * blocks + c * (blocks // 2)), (2, blocks // 2))
    masks = jnp.repeat(masks != 0, half // (blocks // 2), axis=1)
    keep_own = jnp.where(first, masks[0], masks[1])
    keep_far = jnp.where(first, masks[1], masks[0])
    at = jnp.stack([z, c]).astype(jnp.int32)
    part = local_call(
        root_kernel,
        2 * NZ * small,
        width,
        (at, home, one, two, three, four, f12, f43, root_inverse),
        4 * NZ * small * depth * width,
        [pltpu.VMEM((2 * NZ * small, depth), BF)],
    )

    solved = exchange(part.reshape(NX, rows, width), "row").astype(F32).sum(0).astype(BF)
    full = jnp.broadcast_to(solved[None], (NX * NX, rows, width))
    full = exchange(full, ("layer", "row")).reshape(NX * NX * rows, width)
    full_far = to_core(full)
    update = jnp.where(keep_own[None], dot(full, couple_own), 0.0) + jnp.where(
        keep_far[None], dot(full_far, couple_far), 0.0
    )
    update = update.astype(BF).reshape(2 * NZ, rows, half)

    def term(h, d):
        return lax.optimization_barrier(pick(update, 2 * ((z + d) & (NZ - 1)) + h))

    terms = {(h, d): term(h, d) for h in range(2) for d in range(-REACH[h][1], REACH[h][0] + 1)}
    chains = {}
    for step in range(4):
        for h in range(2):
            for way, n in zip((1, -1), REACH[h]):
                if step < n:
                    block = terms[h, way * (n - step)]
                    if step > 0:
                        block = (block.astype(F32) + chains[h, way].astype(F32)).astype(BF)
                    chains[h, way] = along_z(block, way)

    near = []
    for h in range(2):
        base = rhs[h].astype(F32) - terms[h, 0].astype(F32)
        reduced = (base - (chains[h, 1].astype(F32) + chains[h, -1].astype(F32))).astype(BF)
        near.append(put(jnp.zeros((NZ, rows, half), BF), reduced, z))
        chains[h, 1] = chains[h, -1] = reduced
    for step in range(4):
        for h in range(2):
            for way, n in zip((1, -1), REACH[h]):
                if step < n:
                    chains[h, way] = along_z(chains[h, way], way)
                    near[h] = put(near[h], chains[h, way], (z - way * (step + 1)) & (NZ - 1))

    part = ()
    for h, kernel in enumerate((first_kernel, second_kernel)):
        gathered = near[h].reshape(NZ * rows, half)
        far = to_core(gathered)
        part = (
            local_call(
                kernel,
                (h + 1) * NZ * rows,
                width,
                (at, gathered, far, child_inverse[0], *part),
                4 * NZ * rows * half * width,
            ),
        )
    total = exchange(part[0].reshape(NX, 4 * rows, width), "row")
    child = total.astype(F32).sum(0).astype(BF)
    return (solved, child[None])


def solution(mesh):
    in_specs = (
        P(("layer", "col"), "row"),
        P("row", "col"),
        P("layer", "col", "row"),
        P("layer", "row", "col"),
        P("layer", "col", "row"),
        P("layer", None, None),
    )
    out_specs = (P(("layer", "row"), "col"), P("layer", "row", "col"))

    return jax.shard_map(
        on_device, mesh=mesh, in_specs=in_specs, out_specs=out_specs, check_vma=False
    )
```

time: 337 us -> 163 us (0.48)
  waiting for transfers between devices: 305 us -> 29.6 us
  starting transfers between devices: 0.24 us -> 62.4 us
  blocking collectives: 0 us -> 37.6 us
  local copies, waits for them, and re-layouts: 0.09 us -> 13.5 us
  between operations: 14.1 us -> 0.97 us
  matrix products: 16.4 us -> 4.05 us
  Pallas kernels: 0 us -> 6.3 us
  other arithmetic: 0.77 us -> 6.04 us
    all_gather x3 -> x0, waiting for transfers between devices: 136 us -> none  [the longest x1 49 us: on_device(): full_root = lax.all_gather(solved, ('layer', 'row'), axis=0, tiled=True)]
    psum x1 -> x0, waiting for transfers between devices: 121 us -> none  [on_device(): lax.psum(jnp.dot(full_root, masked, preferred_element_type=jnp.float32).a...]
    ppermute x0 -> x40, starting transfers between devices: none -> 58 us  [the longest x28 47.1 us: along_z(): lax.ppermute(x, 'col', [(i, (i + 2 * step) % (2 * NZ)) for i in range(2 *...]
    reduce_scatter x2 -> x0, waiting for transfers between devices: 47 us -> none  [the longest x1 25 us: on_device(): lax.psum_scatter(jnp.dot(reduced, child_inverse[0], preferred_element_typ...]
    all_to_all x0 -> x2, blocking collectives: none -> 37.6 us  [exchange(): return lax.all_to_all(x, axes, 0, 0, tiled=True)]
    ppermute x0 -> x40, waiting for transfers between devices: none -> 22.4 us  [the longest x4 10 us: twisted(): return lax.ppermute(x, 'col', pairs)]
    dot_general x3 -> x2, matrix products: 16.4 us -> 4.05 us  [dot(): return jnp.dot(a, b, preferred_element_type=F32)]
    all_to_all x0 -> x1, waiting for transfers between devices: none -> 7.2 us  [exchange(): return lax.all_to_all(x, axes, 0, 0, tiled=True)]
  transfers between devices with their start and end apart: 6 -> 41, of which waited for: 6 -> 17; matrix products, arithmetic and copies ran while one was open for 0% -> 9% of each run, Pallas kernels for 0% -> 1%
where the time goes in v1:
time: 163 us; the launch traced here: 160 us
  starting transfers between devices  62.4 us (38%)
  blocking collectives  37.6 us (23%)
  waiting for transfers between devices  29.6 us (18%)
  local copies, waits for them, and re-layouts  13.5 us (8%)
  Pallas kernels  6.3 us (4%)
  other arithmetic  6.04 us (4%)
  matrix products  4.05 us (2%)
    ppermute x28, starting transfers between devices, along_z(): lax.ppermute(x, 'col', [(i, (i + 2 * step) % (2 * NZ)) for i in range(2 *...  47.1 us
    all_to_all x2, blocking collectives, exchange(): return lax.all_to_all(x, axes, 0, 0, tiled=True)  37.6 us
    ppermute x4, waiting for transfers between devices, twisted(): return lax.ppermute(x, 'col', pairs)  10 us
    ppermute x4, starting transfers between devices, twisted(): return lax.ppermute(x, 'col', pairs)  9.77 us
    all_to_all x1, waiting for transfers between devices, exchange(): return lax.all_to_all(x, axes, 0, 0, tiled=True)  7.2 us
    ppermute x28, waiting for transfers between devices, along_z(): lax.ppermute(x, 'col', [(i, (i + 2 * step) % (2 * NZ)) for i in range(2 *...  7.08 us
    dynamic_update_slice x14, local copies, waits for them, and re-layouts, put(): return lax.dynamic_update_index_in_dim(x, piece, index, 0)  6.54 us
    pallas_call x3, Pallas kernels, local_call(): pl.pallas_call(kernel, out_shape=jax.ShapeDtypeStruct((rows, width), BF),...  6.3 us
  transfers between devices with their start and end apart: 41, of which 17 were waited for; matrix products, arithmetic and copies ran while one was open for 9% of the time, Pallas kernels for 1%

profile of v1, /device:TPU:8, one launch (start us, length us, event | category | flops | bytes accessed | tf_op | source)
XLA Modules:
  0.0 160.4 jit_solution(556903310232101846)
XLA Ops:
  0.7 3.2 %dynamic-slice_bitcast_fusion = (bf16[512,1024]{1,0:T(8,128)(2,1)}, bf16[512,1024]{1,0:T(8,128)(2,1)}) fusion(bf16[1,512,2048]{2,1,0:T(8,128)(2,1)} %param.10, s32[]{:T(128)S(6)} %select_n.152, s32[]{:T(128)S(6)} %select_n.151), kind=kLoop, calls=%fused_computation.1 | loop fusion | bytes 4194312 | tf_op jit(solution)/shard_map/dynamic_slice | solution.py:130
  8.8 3.3 %collective-permute-start.2 = (bf16[32,2048]{1,0:T(8,128)(2,1)S(1)}, bf16[32,2048]{1,0:T(8,128)(2,1)S(1)}, u32[]{:S(2)}, u32[]{:S(2)}) collective-permute-start(bf16[32,2048]{1,0:T(8,128)(2,1)S(1)} %constant_dynamic-update-slice_fusion.home), channel_id=1, source_target_pairs={{0,4},{1,13},{2,6},{3,15},{4,8},{5,1},{6,10},{7,3},{8,12},{9,5},{1... | collective-permute-start | bytes 393224 | tf_op jit(solution)/shard_map/ppermute | solution.py:26
  12.0 4.5 %collective-permute-start.4 = (bf16[16,2048]{1,0:T(8,128)(2,1)S(1)}, bf16[16,2048]{1,0:T(8,128)(2,1)S(1)}, u32[]{:S(2)}, u32[]{:S(2)}) collective-permute-start(bf16[16,2048]{1,0:T(8,128)(2,1)S(1)} %copy-done.7), channel_id=1, source_target_pairs={{0,8},{1,9},{2,10},{3,11},{4,12},{5,13},{6,14},{7,15},{8,0},{9,1},... | collective-permute-start | bytes 196616 | tf_op jit(solution)/shard_map/ppermute | solution.py:26
  16.6 2.5 %collective-permute-done.2.two = bf16[32,2048]{1,0:T(8,128)(2,1)S(1)} collective-permute-done((bf16[32,2048]{1,0:T(8,128)(2,1)S(1)}, bf16[32,2048]{1,0:T(8,128)(2,1)S(1)}, u32[]{:S(2)}, u32[]{:S(2)}) %collective-permute-start.2) | collective-permute-done | bytes 131104 | tf_op jit(solution)/shard_map/ppermute | solution.py:26
  22.1 5.2 %collective-permute-done.3.three = bf16[32,2048]{1,0:T(8,128)(2,1)S(1)} collective-permute-done((bf16[32,2048]{1,0:T(8,128)(2,1)S(1)}, bf16[32,2048]{1,0:T(8,128)(2,1)S(1)}, u32[]{:S(2)}, u32[]{:S(2)}) %collective-permute-start.3) | collective-permute-done | bytes 131104 | tf_op jit(solution)/shard_map/ppermute | solution.py:26
  32.5 4.4 %all-to-all-start = ((bf16[4,64,512]{2,1,0:T(8,128)(2,1)}), bf16[4,64,512]{2,1,0:T(8,128)(2,1)S(1)}, u32[]{:S(2)}, u32[]{:S(2)}) async-start(bf16[4,64,512]{2,1,0:T(8,128)(2,1)} %bitcast.5), calls=%async_computation | async-start | bytes 524288 | tf_op jit(solution)/shard_map/all_to_all | solution.py:34
  36.9 7.2 %all-to-all-done = bf16[4,64,512]{2,1,0:T(8,128)(2,1)S(1)} async-done(((bf16[4,64,512]{2,1,0:T(8,128)(2,1)}), bf16[4,64,512]{2,1,0:T(8,128)(2,1)S(1)}, u32[]{:S(2)}, u32[]{:S(2)}) %all-to-all-start) | async-done | bytes 262176 | tf_op jit(solution)/shard_map/all_to_all | solution.py:34
  44.9 19.4 %all_to_all.15 = bf16[16,64,512]{2,1,0:T(8,128)(2,1)S(1)} all-to-all(bf16[16,64,512]{2,1,0:T(8,128)(2,1)S(1)} %broadcast_in_dim.85), channel_id=1, replica_groups=mesh['layer'=4,'row'=4,'col'=16] {'layer','row'}, dimensions={0} | all-to-all | bytes 2097152 | tf_op jit(solution)/shard_map/all_to_all | solution.py:34
  67.1 2.8 %add_convert_fusion = bf16[1024,1024]{1,0:T(8,128)(2,1)S(1)} fusion(f32[1024,1024]{1,0:T(8,128)S(1)} %fusion.1, bf16[1024,512]{1,0:T(8,128)(2,1)} %collective-permute-done.9, bf16[512,1024]{1,0:T(8,128)(2,1)} %collective-permute-done.6, pred[1024]{0:T(1024)(128)(4,1)S(1)} %select_n.164, pred[1024]{0:T(1024)(128)(4,1)S(1)} %select_n.160), kind=kOutput, calls=%fused_computation | convolution fusion | flops 1077936128 | bytes 8390656 | tf_op jit(solution)/shard_map/dot_general | solution.py:46
  74.1 3.2 %collective-permute-start.13 = (bf16[64,1024]{1,0:T(8,128)(2,1)S(1)}, bf16[64,1024]{1,0:T(8,128)(2,1)S(1)}, u32[]{:S(2)}, u32[]{:S(2)}) collective-permute-start(bf16[64,1024]{1,0:T(8,128)(2,1)S(1)} %get-tuple-element.22), channel_id=1, source_target_pairs={{0,14},{1,15},{2,0},{3,1},{4,2},{5,3},{6,4},{7,5},{8,6},{9,7},{10,... | collective-permute-start | bytes 393224 | tf_op jit(solution)/shard_map/ppermute | solution.py:30
  78.0 3.1 %collective-permute-start.30 = (bf16[64,1024]{1,0:T(8,128)(2,1)S(1)}, bf16[64,1024]{1,0:T(8,128)(2,1)S(1)}, u32[]{:S(2)}, u32[]{:S(2)}) collective-permute-start(bf16[64,1024]{1,0:T(8,128)(2,1)S(1)} %add_convert_fusion.2), channel_id=1, source_target_pairs={{0,14},{1,15},{2,0},{3,1},{4,2},{5,3},{6,4},{7,5},{8,6},{9,7},{10,... | collective-permute-start | bytes 393224 | tf_op jit(solution)/shard_map/ppermute | solution.py:30
  81.3 3.3 %collective-permute-start.14 = (bf16[64,1024]{1,0:T(8,128)(2,1)S(1)}, bf16[64,1024]{1,0:T(8,128)(2,1)S(1)}, u32[]{:S(2)}, u32[]{:S(2)}) collective-permute-start(bf16[64,1024]{1,0:T(8,128)(2,1)S(1)} %add_convert_fusion.8), channel_id=1, source_target_pairs={{0,14},{1,15},{2,0},{3,1},{4,2},{5,3},{6,4},{7,5},{8,6},{9,7},{10,... | collective-permute-start | bytes 393224 | tf_op jit(solution)/shard_map/ppermute | solution.py:30
  84.8 3.3 %collective-permute-start.31 = (bf16[64,1024]{1,0:T(8,128)(2,1)S(1)}, bf16[64,1024]{1,0:T(8,128)(2,1)S(1)}, u32[]{:S(2)}, u32[]{:S(2)}) collective-permute-start(bf16[64,1024]{1,0:T(8,128)(2,1)S(1)} %add_convert_fusion.1), channel_id=1, source_target_pairs={{0,14},{1,15},{2,0},{3,1},{4,2},{5,3},{6,4},{7,5},{8,6},{9,7},{10,... | collective-permute-start | bytes 393224 | tf_op jit(solution)/shard_map/ppermute | solution.py:30
  88.5 3.6 %collective-permute-start.15 = (bf16[64,1024]{1,0:T(8,128)(2,1)S(1)}, bf16[64,1024]{1,0:T(8,128)(2,1)S(1)}, u32[]{:S(2)}, u32[]{:S(2)}) collective-permute-start(bf16[64,1024]{1,0:T(8,128)(2,1)S(1)} %add_convert_fusion.7), channel_id=1, source_target_pairs={{0,14},{1,15},{2,0},{3,1},{4,2},{5,3},{6,4},{7,5},{8,6},{9,7},{10,... | collective-permute-start | bytes 393224 | tf_op jit(solution)/shard_map/ppermute | solution.py:30
  94.6 3.7 %collective-permute-start.16 = (bf16[64,1024]{1,0:T(8,128)(2,1)S(1)}, bf16[64,1024]{1,0:T(8,128)(2,1)S(1)}, u32[]{:S(2)}, u32[]{:S(2)}) collective-permute-start(bf16[64,1024]{1,0:T(8,128)(2,1)S(1)} %add_convert_fusion.6), channel_id=1, source_target_pairs={{0,14},{1,15},{2,0},{3,1},{4,2},{5,3},{6,4},{7,5},{8,6},{9,7},{10,... | collective-permute-start | bytes 393224 | tf_op jit(solution)/shard_map/ppermute | solution.py:30
  99.5 3.2 %collective-permute-start.33 = (bf16[64,1024]{1,0:T(8,128)(2,1)}, bf16[64,1024]{1,0:T(8,128)(2,1)}, u32[]{:S(2)}, u32[]{:S(2)}) collective-permute-start(bf16[64,1024]{1,0:T(8,128)(2,1)} %get-tuple-element.11), channel_id=1, source_target_pairs={{0,14},{1,15},{2,0},{3,1},{4,2},{5,3},{6,4},{7,5},{8,6},{9,7},{10,... | collective-permute-start | bytes 393224 | tf_op jit(solution)/shard_map/ppermute | solution.py:30
  105.6 3.2 %collective-permute-start.18 = (bf16[64,1024]{1,0:T(8,128)(2,1)}, bf16[64,1024]{1,0:T(8,128)(2,1)S(1)}, u32[]{:S(2)}, u32[]{:S(2)}) collective-permute-start(bf16[64,1024]{1,0:T(8,128)(2,1)} %get-tuple-element.13), channel_id=1, source_target_pairs={{0,14},{1,15},{2,0},{3,1},{4,2},{5,3},{6,4},{7,5},{8,6},{9,7},{10,... | collective-permute-start | bytes 393224 | tf_op jit(solution)/shard_map/ppermute | solution.py:30
  108.8 3.2 %collective-permute-start.35 = (bf16[64,1024]{1,0:T(8,128)(2,1)}, bf16[64,1024]{1,0:T(8,128)(2,1)S(1)}, u32[]{:S(2)}, u32[]{:S(2)}) collective-permute-start(bf16[64,1024]{1,0:T(8,128)(2,1)} %collective-permute-done.33), channel_id=1, source_target_pairs={{0,14},{1,15},{2,0},{3,1},{4,2},{5,3},{6,4},{7,5},{8,6},{9,7},{10,... | collective-permute-start | bytes 393224 | tf_op jit(solution)/shard_map/ppermute | solution.py:30
  114.6 3.2 %collective-permute-start.20 = (bf16[64,1024]{1,0:T(8,128)(2,1)S(1)}, bf16[64,1024]{1,0:T(8,128)(2,1)S(1)}, u32[]{:S(2)}, u32[]{:S(2)}) collective-permute-start(bf16[64,1024]{1,0:T(8,128)(2,1)S(1)} %collective-permute-done.18), channel_id=1, source_target_pairs={{0,14},{1,15},{2,0},{3,1},{4,2},{5,3},{6,4},{7,5},{8,6},{9,7},{10,... | collective-permute-start | bytes 393224 | tf_op jit(solution)/shard_map/ppermute | solution.py:30
  119.4 3.2 %collective-permute-start.37 = (bf16[64,1024]{1,0:T(8,128)(2,1)S(1)}, bf16[64,1024]{1,0:T(8,128)(2,1)S(1)}, u32[]{:S(2)}, u32[]{:S(2)}) collective-permute-start(bf16[64,1024]{1,0:T(8,128)(2,1)S(1)} %collective-permute-done.35), channel_id=1, source_target_pairs={{0,14},{1,15},{2,0},{3,1},{4,2},{5,3},{6,4},{7,5},{8,6},{9,7},{10,... | collective-permute-start | bytes 393224 | tf_op jit(solution)/shard_map/ppermute | solution.py:30
  123.4 3.2 %collective-permute-start.22 = (bf16[64,1024]{1,0:T(8,128)(2,1)S(1)}, bf16[64,1024]{1,0:T(8,128)(2,1)S(1)}, u32[]{:S(2)}, u32[]{:S(2)}) collective-permute-start(bf16[64,1024]{1,0:T(8,128)(2,1)S(1)} %collective-permute-done.20), channel_id=1, source_target_pairs={{0,14},{1,15},{2,0},{3,1},{4,2},{5,3},{6,4},{7,5},{8,6},{9,7},{10,... | collective-permute-start | bytes 393224 | tf_op jit(solution)/shard_map/ppermute | solution.py:30
  129.1 3.7 %collective-permute-start.23 = (bf16[64,1024]{1,0:T(8,128)(2,1)S(1)}, bf16[64,1024]{1,0:T(8,128)(2,1)S(1)}, u32[]{:S(2)}, u32[]{:S(2)}) collective-permute-start(bf16[64,1024]{1,0:T(8,128)(2,1)S(1)} %collective-permute-done.22), channel_id=1, source_target_pairs={{0,14},{1,15},{2,0},{3,1},{4,2},{5,3},{6,4},{7,5},{8,6},{9,7},{10,... | collective-permute-start | bytes 393224 | tf_op jit(solution)/shard_map/ppermute | solution.py:30
  138.8 2.5 %shard_map.79 = bf16[1024,512]{1,0:T(8,128)(2,1)S(1)} custom-call(s32[2]{0:T(128)S(1)} %pad_add_fusion.at, bf16[512,1024]{1,0:T(8,128)(2,1)} %bitcast.27.near, bf16[512,1024]{1,0:T(8,128)(2,1)S(1)} %collective-permute-done.24.far, bf16[2048,512]{1,0:T(8,128)(2,1)S(1)} %bitcast.98, bf16[512,512]{1,0:T(8,128)(2,1)S(1)} %shard_map.78.before), custom_call_target="tpu_custom_call" | custom-call | flops 1073741824 | bytes 5767176 | tf_op jit(solution)/shard_map/pallas_call | solution.py:97
  141.3 18.2 %all_to_all.16 = bf16[4,256,512]{2,1,0:T(8,128)(2,1)S(1)} all-to-all(bf16[4,256,512]{2,1,0:T(8,128)(2,1)S(1)} %bitcast.101), channel_id=1, replica_groups=mesh['layer'=4,'row'=4,'col'=16] {'row'}, dimensions={0} | all-to-all | bytes 2097152 | tf_op jit(solution)/shard_map/all_to_all | solution.py:34
  (126 shorter events, 43.0 us)
Async XLA Ops:
  3.8 26.6 %collective-permute-start.6 = (bf16[512,1024]{1,0:T(8,128)(2,1)}, bf16[512,1024]{1,0:T(8,128)(2,1)}, u32[]{:S(2)}, u32[]{:S(2)}) collective-permute-start(bf16[512,1024]{1,0:T(8,128)(2,1)} %get-tuple-element.31), channel_id=1, source_target_pairs={{0,1},{1,0},{2,3},{3,2},{4,5},{5,4},{6,7},{7,6},{8,9},{9,8},{10,11... | collective-permute-start | bytes 3145736 | tf_op jit(solution)/shard_map/ppermute | solution.py:18
  6.8 9.8 %collective-permute-start.1 = (bf16[32,2048]{1,0:T(8,128)(2,1)S(1)}, bf16[32,2048]{1,0:T(8,128)(2,1)S(1)}, u32[]{:S(2)}, u32[]{:S(2)}) collective-permute-start(bf16[32,2048]{1,0:T(8,128)(2,1)S(1)} %constant_dynamic-update-slice_fusion.home), channel_id=1, source_target_pairs={{0,2},{1,15},{2,4},{3,1},{4,6},{5,3},{6,8},{7,5},{8,10},{9,7},{10,... | collective-permute-start | bytes 393224 | tf_op jit(solution)/shard_map/ppermute | solution.py:26
  8.8 10.4 %collective-permute-start.2 = (bf16[32,2048]{1,0:T(8,128)(2,1)S(1)}, bf16[32,2048]{1,0:T(8,128)(2,1)S(1)}, u32[]{:S(2)}, u32[]{:S(2)}) collective-permute-start(bf16[32,2048]{1,0:T(8,128)(2,1)S(1)} %constant_dynamic-update-slice_fusion.home), channel_id=1, source_target_pairs={{0,4},{1,13},{2,6},{3,15},{4,8},{5,1},{6,10},{7,3},{8,12},{9,5},{1... | collective-permute-start | bytes 393224 | tf_op jit(solution)/shard_map/ppermute | solution.py:26
  12.0 10.1 %collective-permute-start.4 = (bf16[16,2048]{1,0:T(8,128)(2,1)S(1)}, bf16[16,2048]{1,0:T(8,128)(2,1)S(1)}, u32[]{:S(2)}, u32[]{:S(2)}) collective-permute-start(bf16[16,2048]{1,0:T(8,128)(2,1)S(1)} %copy-done.7), channel_id=1, source_target_pairs={{0,8},{1,9},{2,10},{3,11},{4,12},{5,13},{6,14},{7,15},{8,0},{9,1},... | collective-permute-start | bytes 196616 | tf_op jit(solution)/shard_map/ppermute | solution.py:26
  16.5 10.8 %collective-permute-start.3 = (bf16[32,2048]{1,0:T(8,128)(2,1)S(1)}, bf16[32,2048]{1,0:T(8,128)(2,1)S(1)}, u32[]{:S(2)}, u32[]{:S(2)}) collective-permute-start(bf16[32,2048]{1,0:T(8,128)(2,1)S(1)} %constant_dynamic-update-slice_fusion.home), channel_id=1, source_target_pairs={{0,6},{1,11},{2,8},{3,13},{4,10},{5,15},{6,12},{7,1},{8,14},{9,3},... | collective-permute-start | bytes 393224 | tf_op jit(solution)/shard_map/ppermute | solution.py:26
  19.8 10.6 %collective-permute-start.5 = (bf16[64,2048]{1,0:T(8,128)(2,1)}, bf16[64,2048]{1,0:T(8,128)(2,1)S(1)}, u32[]{:S(2)}, u32[]{:S(2)}) collective-permute-start(bf16[64,2048]{1,0:T(8,128)(2,1)} %pad_maximum_fusion), channel_id=1, source_target_pairs={{0,1},{1,0},{2,3},{3,2},{4,5},{5,4},{6,7},{7,6},{8,9},{9,8},{10,11... | collective-permute-start | bytes 786440 | tf_op jit(solution)/shard_map/ppermute | solution.py:18
  32.5 11.6 %all-to-all-start = ((bf16[4,64,512]{2,1,0:T(8,128)(2,1)}), bf16[4,64,512]{2,1,0:T(8,128)(2,1)S(1)}, u32[]{:S(2)}, u32[]{:S(2)}) async-start(bf16[4,64,512]{2,1,0:T(8,128)(2,1)} %bitcast.5), calls=%async_computation | async-start | bytes 524288 | tf_op jit(solution)/shard_map/all_to_all | solution.py:34
  74.1 7.2 %collective-permute-start.13 = (bf16[64,1024]{1,0:T(8,128)(2,1)S(1)}, bf16[64,1024]{1,0:T(8,128)(2,1)S(1)}, u32[]{:S(2)}, u32[]{:S(2)}) collective-permute-start(bf16[64,1024]{1,0:T(8,128)(2,1)S(1)} %get-tuple-element.22), channel_id=1, source_target_pairs={{0,14},{1,15},{2,0},{3,1},{4,2},{5,3},{6,4},{7,5},{8,6},{9,7},{10,... | collective-permute-start | bytes 393224 | tf_op jit(solution)/shard_map/ppermute | solution.py:30
  81.2 7.1 %collective-permute-start.11 = (bf16[64,1024]{1,0:T(8,128)(2,1)S(1)}, bf16[64,1024]{1,0:T(8,128)(2,1)S(1)}, u32[]{:S(2)}, u32[]{:S(2)}) collective-permute-start(bf16[64,1024]{1,0:T(8,128)(2,1)S(1)} %add_convert_fusion.10), channel_id=1, source_target_pairs={{0,2},{1,3},{2,4},{3,5},{4,6},{5,7},{6,8},{7,9},{8,10},{9,11},{10,... | collective-permute-start | bytes 393224 | tf_op jit(solution)/shard_map/ppermute | solution.py:30
  84.7 7.6 %collective-permute-start.27 = (bf16[64,1024]{1,0:T(8,128)(2,1)S(1)}, bf16[64,1024]{1,0:T(8,128)(2,1)S(1)}, u32[]{:S(2)}, u32[]{:S(2)}) collective-permute-start(bf16[64,1024]{1,0:T(8,128)(2,1)S(1)} %add_convert_fusion.4), channel_id=1, source_target_pairs={{0,2},{1,3},{2,4},{3,5},{4,6},{5,7},{6,8},{7,9},{8,10},{9,11},{10,... | collective-permute-start | bytes 393224 | tf_op jit(solution)/shard_map/ppermute | solution.py:30
  84.8 13.6 %collective-permute-start.31 = (bf16[64,1024]{1,0:T(8,128)(2,1)S(1)}, bf16[64,1024]{1,0:T(8,128)(2,1)S(1)}, u32[]{:S(2)}, u32[]{:S(2)}) collective-permute-start(bf16[64,1024]{1,0:T(8,128)(2,1)S(1)} %add_convert_fusion.1), channel_id=1, source_target_pairs={{0,14},{1,15},{2,0},{3,1},{4,2},{5,3},{6,4},{7,5},{8,6},{9,7},{10,... | collective-permute-start | bytes 393224 | tf_op jit(solution)/shard_map/ppermute | solution.py:30
  88.4 14.4 %collective-permute-start.12 = (bf16[64,1024]{1,0:T(8,128)(2,1)S(1)}, bf16[64,1024]{1,0:T(8,128)(2,1)S(1)}, u32[]{:S(2)}, u32[]{:S(2)}) collective-permute-start(bf16[64,1024]{1,0:T(8,128)(2,1)S(1)} %add_convert_fusion.9), channel_id=1, source_target_pairs={{0,2},{1,3},{2,4},{3,5},{4,6},{5,7},{6,8},{7,9},{8,10},{9,11},{10,... | collective-permute-start | bytes 393224 | tf_op jit(solution)/shard_map/ppermute | solution.py:30
  94.6 8.1 %collective-permute-start.16 = (bf16[64,1024]{1,0:T(8,128)(2,1)S(1)}, bf16[64,1024]{1,0:T(8,128)(2,1)S(1)}, u32[]{:S(2)}, u32[]{:S(2)}) collective-permute-start(bf16[64,1024]{1,0:T(8,128)(2,1)S(1)} %add_convert_fusion.6), channel_id=1, source_target_pairs={{0,14},{1,15},{2,0},{3,1},{4,2},{5,3},{6,4},{7,5},{8,6},{9,7},{10,... | collective-permute-start | bytes 393224 | tf_op jit(solution)/shard_map/ppermute | solution.py:30
  99.5 9.3 %collective-permute-start.32 = (bf16[64,1024]{1,0:T(8,128)(2,1)}, bf16[64,1024]{1,0:T(8,128)(2,1)}, u32[]{:S(2)}, u32[]{:S(2)}) collective-permute-start(bf16[64,1024]{1,0:T(8,128)(2,1)} %get-tuple-element.11), channel_id=1, source_target_pairs={{0,2},{1,3},{2,4},{3,5},{4,6},{5,7},{6,8},{7,9},{8,10},{9,11},{10,... | collective-permute-start | bytes 393224 | tf_op jit(solution)/shard_map/ppermute | solution.py:30
  99.5 9.3 %collective-permute-start.33 = (bf16[64,1024]{1,0:T(8,128)(2,1)}, bf16[64,1024]{1,0:T(8,128)(2,1)}, u32[]{:S(2)}, u32[]{:S(2)}) collective-permute-start(bf16[64,1024]{1,0:T(8,128)(2,1)} %get-tuple-element.11), channel_id=1, source_target_pairs={{0,14},{1,15},{2,0},{3,1},{4,2},{5,3},{6,4},{7,5},{8,6},{9,7},{10,... | collective-permute-start | bytes 393224 | tf_op jit(solution)/shard_map/ppermute | solution.py:30
  105.6 7.4 %collective-permute-start.17 = (bf16[64,1024]{1,0:T(8,128)(2,1)}, bf16[64,1024]{1,0:T(8,128)(2,1)S(1)}, u32[]{:S(2)}, u32[]{:S(2)}) collective-permute-start(bf16[64,1024]{1,0:T(8,128)(2,1)} %get-tuple-element.13), channel_id=1, source_target_pairs={{0,2},{1,3},{2,4},{3,5},{4,6},{5,7},{6,8},{7,9},{8,10},{9,11},{10,... | collective-permute-start | bytes 393224 | tf_op jit(solution)/shard_map/ppermute | solution.py:30
  105.6 9.0 %collective-permute-start.18 = (bf16[64,1024]{1,0:T(8,128)(2,1)}, bf16[64,1024]{1,0:T(8,128)(2,1)S(1)}, u32[]{:S(2)}, u32[]{:S(2)}) collective-permute-start(bf16[64,1024]{1,0:T(8,128)(2,1)} %get-tuple-element.13), channel_id=1, source_target_pairs={{0,14},{1,15},{2,0},{3,1},{4,2},{5,3},{6,4},{7,5},{8,6},{9,7},{10,... | collective-permute-start | bytes 393224 | tf_op jit(solution)/shard_map/ppermute | solution.py:30
  108.8 10.6 %collective-permute-start.34 = (bf16[64,1024]{1,0:T(8,128)(2,1)}, bf16[64,1024]{1,0:T(8,128)(2,1)S(1)}, u32[]{:S(2)}, u32[]{:S(2)}) collective-permute-start(bf16[64,1024]{1,0:T(8,128)(2,1)} %collective-permute-done.32), channel_id=1, source_target_pairs={{0,2},{1,3},{2,4},{3,5},{4,6},{5,7},{6,8},{7,9},{8,10},{9,11},{10,... | collective-permute-start | bytes 393224 | tf_op jit(solution)/shard_map/ppermute | solution.py:30
  108.8 10.6 %collective-permute-start.35 = (bf16[64,1024]{1,0:T(8,128)(2,1)}, bf16[64,1024]{1,0:T(8,128)(2,1)S(1)}, u32[]{:S(2)}, u32[]{:S(2)}) collective-permute-start(bf16[64,1024]{1,0:T(8,128)(2,1)} %collective-permute-done.33), channel_id=1, source_target_pairs={{0,14},{1,15},{2,0},{3,1},{4,2},{5,3},{6,4},{7,5},{8,6},{9,7},{10,... | collective-permute-start | bytes 393224 | tf_op jit(solution)/shard_map/ppermute | solution.py:30
  113.0 9.7 %collective-permute-start.19 = (bf16[64,1024]{1,0:T(8,128)(2,1)S(1)}, bf16[64,1024]{1,0:T(8,128)(2,1)S(1)}, u32[]{:S(2)}, u32[]{:S(2)}) collective-permute-start(bf16[64,1024]{1,0:T(8,128)(2,1)S(1)} %collective-permute-done.17), channel_id=1, source_target_pairs={{0,2},{1,3},{2,4},{3,5},{4,6},{5,7},{6,8},{7,9},{8,10},{9,11},{10,... | collective-permute-start | bytes 393224 | tf_op jit(solution)/shard_map/ppermute | solution.py:30
  114.6 8.7 %collective-permute-start.20 = (bf16[64,1024]{1,0:T(8,128)(2,1)S(1)}, bf16[64,1024]{1,0:T(8,128)(2,1)S(1)}, u32[]{:S(2)}, u32[]{:S(2)}) collective-permute-start(bf16[64,1024]{1,0:T(8,128)(2,1)S(1)} %collective-permute-done.18), channel_id=1, source_target_pairs={{0,14},{1,15},{2,0},{3,1},{4,2},{5,3},{6,4},{7,5},{8,6},{9,7},{10,... | collective-permute-start | bytes 393224 | tf_op jit(solution)/shard_map/ppermute | solution.py:30
  119.4 7.8 %collective-permute-start.36 = (bf16[64,1024]{1,0:T(8,128)(2,1)S(1)}, bf16[64,1024]{1,0:T(8,128)(2,1)S(1)}, u32[]{:S(2)}, u32[]{:S(2)}) collective-permute-start(bf16[64,1024]{1,0:T(8,128)(2,1)S(1)} %collective-permute-done.34), channel_id=1, source_target_pairs={{0,2},{1,3},{2,4},{3,5},{4,6},{5,7},{6,8},{7,9},{8,10},{9,11},{10,... | collective-permute-start | bytes 393224 | tf_op jit(solution)/shard_map/ppermute | solution.py:30
  119.4 14.7 %collective-permute-start.37 = (bf16[64,1024]{1,0:T(8,128)(2,1)S(1)}, bf16[64,1024]{1,0:T(8,128)(2,1)S(1)}, u32[]{:S(2)}, u32[]{:S(2)}) collective-permute-start(bf16[64,1024]{1,0:T(8,128)(2,1)S(1)} %collective-permute-done.35), channel_id=1, source_target_pairs={{0,14},{1,15},{2,0},{3,1},{4,2},{5,3},{6,4},{7,5},{8,6},{9,7},{10,... | collective-permute-start | bytes 393224 | tf_op jit(solution)/shard_map/ppermute | solution.py:30
  122.7 10.1 %collective-permute-start.21 = (bf16[64,1024]{1,0:T(8,128)(2,1)S(1)}, bf16[64,1024]{1,0:T(8,128)(2,1)S(1)}, u32[]{:S(2)}, u32[]{:S(2)}) collective-permute-start(bf16[64,1024]{1,0:T(8,128)(2,1)S(1)} %collective-permute-done.19), channel_id=1, source_target_pairs={{0,2},{1,3},{2,4},{3,5},{4,6},{5,7},{6,8},{7,9},{8,10},{9,11},{10,... | collective-permute-start | bytes 393224 | tf_op jit(solution)/shard_map/ppermute | solution.py:30
  (25 other events, 293.2 us)

commit v2 on v1

--- a/solution.py
+++ b/solution.py
@@ -30,6 +30,10 @@
     return lax.ppermute(x, "col", [(i, (i + 2 * step) % (2 * NZ)) for i in range(2 * NZ)])
 
 
+def along_x(x, step):
+    return lax.ppermute(x, "row", [(i, (i + step) % NX) for i in range(NX)])
+
+
 def exchange(x, axes):
     return lax.all_to_all(x, axes, 0, 0, tiled=True)
 
@@ -46,7 +50,7 @@
     return jnp.dot(a, b, preferred_element_type=F32)
 
 
-def root_kernel(at, home, one, two, three, four, f12, f34, a, out, x):
+def root_kernel(at, home, one, two, three, four, others, a, out, x):
     z, c = at[0], at[1]
     sign = 1 - 2 * c
     n = home.shape[0]
@@ -65,10 +69,9 @@
     pair(two, 0, z - 2 * sign, c)
     pair(three, 0, z - 3 * sign, c)
     place(four[...], z + 4, c)
-    pair(f12, 0, z + sign, 1 - c)
-    pair(f12, n, z + 2 * sign, 1 - c)
-    pair(f34, 0, z + 3 * sign, 1 - c)
-    place(f34[n:, :], z + 4, 1 - c)
+    for i in range(3):
+        pair(others, i * n, z + (i + 1) * sign, 1 - c)
+    place(others[3 * n :, :], z + 4, 1 - c)
     out[...] = dot(x[...], a[...]).astype(BF)
 
 
@@ -83,27 +86,31 @@
     out[...] = child_product(at[1], near, far, inverse)
 
 
-def second_kernel(at, near, far, inverse, before, out):
+def second_kernel(at, near, far, inverse, before, *refs):
+    outs, whole = refs[:NX], refs[NX]
     block = child_product(at[1], near, far, inverse)
     n = before.shape[0] // NZ
     for i in range(NZ):
-        out[2 * i * n : (2 * i + 1) * n, :] = before[i * n : (i + 1) * n, :]
-        out[(2 * i + 1) * n : (2 * i + 2) * n, :] = block[i * n : (i + 1) * n, :]
-
-
-def local_call(kernel, rows, width, inputs, flops, scratch=()):
+        whole[2 * i * n : (2 * i + 1) * n, :] = before[i * n : (i + 1) * n, :]
+        whole[(2 * i + 1) * n : (2 * i + 2) * n, :] = block[i * n : (i + 1) * n, :]
+    size = whole.shape[0] // NX
+    for d in range(NX):
+        start = pl.multiple_of(((at[2] + d) & (NX - 1)) * size, size)
+        outs[d][...] = whole[pl.ds(start, size), :]
+
+
+def local_call(kernel, shapes, inputs, flops, scratch=()):
     vmem = pl.BlockSpec(memory_space=pltpu.VMEM)
-    size = sum(x.size * x.dtype.itemsize for x in inputs)
+    shapes = [jax.ShapeDtypeStruct(shape, BF) for shape in shapes]
+    size = sum(x.size * x.dtype.itemsize for x in (*inputs, *shapes))
     return pl.pallas_call(
         kernel,
-        out_shape=jax.ShapeDtypeStruct((rows, width), BF),
+        out_shape=shapes,
         in_specs=[pl.BlockSpec(memory_space=pltpu.SMEM)] + [vmem] * (len(inputs) - 1),
-        out_specs=vmem,
+        out_specs=[vmem] * len(shapes),
         scratch_shapes=scratch,
         compiler_params=pltpu.CompilerParams(vmem_limit_bytes=16 * 2**20),
-        cost_estimate=pl.CostEstimate(
-            flops=flops, bytes_accessed=size + 2 * rows * width, transcendentals=0
-        ),
+        cost_estimate=pl.CostEstimate(flops=flops, bytes_accessed=size, transcendentals=0),
     )(*inputs)
 
 
@@ -128,26 +135,29 @@
     two = twisted(home, 2)
     one = twisted(home, 1)
     couple_own = lax.dynamic_slice(off_diagonal[0], (0, c * half), (height, half))
-    couple_out = lax.dynamic_slice(off_diagonal[0], (0, (1 - c) * half), (height, half))
     rhs_own = lax.dynamic_slice(child_rhs[0], (0, c * half), (rows, half))
-    rhs_out = lax.dynamic_slice(child_rhs[0], (0, (1 - c) * half), (rows, half))
-    f43 = to_core(jnp.concatenate([three, four]))
-    f12 = to_core(jnp.concatenate([one, two]))
-    couple_far, rhs_far = to_core(couple_out), to_core(rhs_out)
-    f12, couple_far, rhs_far, couple_own = lax.optimization_barrier(
-        (f12, couple_far, rhs_far, couple_own)
-    )
-    rhs = (jnp.where(first, rhs_own, rhs_far), jnp.where(first, rhs_far, rhs_own))
+    away = jnp.concatenate(
+        [
+            lax.dynamic_slice(off_diagonal[0], (0, (1 - c) * half), (height, half)),
+            lax.dynamic_slice(child_rhs[0], (0, (1 - c) * half), (rows, half)),
+        ]
+    )
+    away = to_core(away)
+    others = to_core(jnp.concatenate([one, two, three, four]))
+    others, away, couple_own, rhs_own = lax.optimization_barrier((others, away, couple_own, rhs_own))
+    couple_far, rhs_far = away[:height], away[height:]
+    rhs = lax.optimization_barrier(
+        (jnp.where(first, rhs_own, rhs_far), jnp.where(first, rhs_far, rhs_own))
+    )
     masks = lax.dynamic_slice(pattern[0], (2 * z, r * blocks + c * (blocks // 2)), (2, blocks // 2))
     masks = jnp.repeat(masks != 0, half // (blocks // 2), axis=1)
     keep_own = jnp.where(first, masks[0], masks[1])
     keep_far = jnp.where(first, masks[1], masks[0])
-    at = jnp.stack([z, c]).astype(jnp.int32)
-    part = local_call(
+    at = jnp.stack([z, c, r]).astype(jnp.int32)
+    (part,) = local_call(
         root_kernel,
-        2 * NZ * small,
-        width,
-        (at, home, one, two, three, four, f12, f43, root_inverse),
+        [(2 * NZ * small, width)],
+        (at, home, one, two, three, four, others, root_inverse),
         4 * NZ * small * depth * width,
         [pltpu.VMEM((2 * NZ * small, depth), BF)],
     )
@@ -156,9 +166,9 @@
     full = jnp.broadcast_to(solved[None], (NX * NX, rows, width))
     full = exchange(full, ("layer", "row")).reshape(NX * NX * rows, width)
     full_far = to_core(full)
-    update = jnp.where(keep_own[None], dot(full, couple_own), 0.0) + jnp.where(
-        keep_far[None], dot(full_far, couple_far), 0.0
-    )
+    update = lax.optimization_barrier(
+        jnp.where(keep_own[None], dot(full, couple_own), 0.0).astype(BF)
+    ).astype(F32) + jnp.where(keep_far[None], dot(full_far, couple_far), 0.0)
     update = update.astype(BF).reshape(2 * NZ, rows, half)
 
     def term(h, d):
@@ -177,7 +187,7 @@
 
     near = []
     for h in range(2):
-        base = rhs[h].astype(F32) - terms[h, 0].astype(F32)
+        base = lax.optimization_barrier(rhs[h].astype(F32) - terms[h, 0].astype(F32))
         reduced = (base - (chains[h, 1].astype(F32) + chains[h, -1].astype(F32))).astype(BF)
         near.append(put(jnp.zeros((NZ, rows, half), BF), reduced, z))
         chains[h, 1] = chains[h, -1] = reduced
@@ -188,21 +198,25 @@
                     chains[h, way] = along_z(chains[h, way], way)
                     near[h] = put(near[h], chains[h, way], (z - way * (step + 1)) & (NZ - 1))
 
-    part = ()
-    for h, kernel in enumerate((first_kernel, second_kernel)):
+    calls = (
+        (first_kernel, [(NZ * rows, width)], ()),
+        (second_kernel, [(4 * rows, width)] * NX, [pltpu.VMEM((2 * NZ * rows, width), BF)]),
+    )
+    parts = ()
+    for h, (kernel, shapes, scratch) in enumerate(calls):
         gathered = near[h].reshape(NZ * rows, half)
         far = to_core(gathered)
-        part = (
-            local_call(
-                kernel,
-                (h + 1) * NZ * rows,
-                width,
-                (at, gathered, far, child_inverse[0], *part),
-                4 * NZ * rows * half * width,
-            ),
+        parts = local_call(
+            kernel,
+            shapes,
+            (at, gathered, far, child_inverse[0], *parts),
+            4 * NZ * rows * half * width,
+            scratch,
         )
-    total = exchange(part[0].reshape(NX, 4 * rows, width), "row")
-    child = total.astype(F32).sum(0).astype(BF)
+    total = parts[0].astype(F32)
+    for step in (2, 1, 3):
+        total = total + along_x(parts[step], step).astype(F32)
+    child = total.astype(BF)
     return (solved, child[None])
 
 

time: 163 us -> 158 us (0.969)
  the two profiles are of different devices: /device:TPU:8 before, /device:TPU:1 now
where the time goes in v2:
time: 158 us; the launch traced here: 157 us
  starting transfers between devices  73.7 us (47%)
  waiting for transfers between devices  36.9 us (23%)
  blocking collectives  20 us (13%)
  local copies, waits for them, and re-layouts  9.56 us (6%)
  other arithmetic  6.47 us (4%)
  Pallas kernels  5.67 us (4%)
  matrix products  4.05 us (3%)
    ppermute x28, starting transfers between devices, along_z(): lax.ppermute(x, 'col', [(i, (i + 2 * step) % (2 * NZ)) for i in range(2 *...  39.6 us
    all_to_all x1, blocking collectives, exchange(): return lax.all_to_all(x, axes, 0, 0, tiled=True)  20 us
    ppermute x6, starting transfers between devices, to_core(): return lax.ppermute(x, 'col', [(i, i ^ 1) for i in range(2 * NZ)])  16.7 us
    ppermute x3, waiting for transfers between devices, along_x(): return lax.ppermute(x, 'row', [(i, (i + step) % NX) for i in range(NX)])  12.1 us
    ppermute x4, starting transfers between devices, twisted(): return lax.ppermute(x, 'col', pairs)  9.97 us
    ppermute x28, waiting for transfers between devices, along_z(): lax.ppermute(x, 'col', [(i, (i + 2 * step) % (2 * NZ)) for i in range(2 *...  6.69 us
    ppermute x6, waiting for transfers between devices, to_core(): return lax.ppermute(x, 'col', [(i, i ^ 1) for i in range(2 * NZ)])  6.32 us
    ppermute x4, waiting for transfers between devices, twisted(): return lax.ppermute(x, 'col', pairs)  5.93 us
  transfers between devices with their start and end apart: 42, of which 13 were waited for; matrix products, arithmetic and copies ran while one was open for 7% of the time, Pallas kernels for 1%

profile of v2, /device:TPU:1, one launch (start us, length us, event | category | flops | bytes accessed | tf_op | source)
XLA Modules:
  0.0 157.3 jit_solution(18153406257023399502)
XLA Ops:
  0.6 2.7 %dynamic-slice_bitcast_fusion = (bf16[512,1024]{1,0:T(8,128)(2,1)}, bf16[512,1024]{1,0:T(8,128)(2,1)S(1)}) fusion(bf16[1,512,2048]{2,1,0:T(8,128)(2,1)} %param.10, s32[]{:T(128)S(6)} %select_n.152, s32[]{:T(128)S(6)} %select_n.151), kind=kLoop, calls=%fused_computation.4 | loop fusion | bytes 4194312 | tf_op jit(solution)/shard_map/dynamic_slice | solution.py:137
  4.5 3.2 %collective-permute-start.6 = (bf16[576,1024]{1,0:T(8,128)(2,1)}, bf16[576,1024]{1,0:T(8,128)(2,1)}, u32[]{:S(2)}, u32[]{:S(2)}) collective-permute-start(bf16[576,1024]{1,0:T(8,128)(2,1)} %pad_maximum_fusion), channel_id=1, source_target_pairs={{0,1},{1,0},{2,3},{3,2},{4,5},{5,4},{6,7},{7,6},{8,9},{9,8},{10,11... | collective-permute-start | bytes 3538952 | tf_op jit(solution)/shard_map/ppermute | solution.py:18
  7.8 2.8 %collective-permute-done = bf16[16,2048]{1,0:T(8,128)(2,1)S(1)} collective-permute-done((bf16[16,2048]{1,0:T(8,128)(2,1)S(1)}, bf16[16,2048]{1,0:T(8,128)(2,1)S(1)}, u32[]{:S(2)}, u32[]{:S(2)}) %collective-permute-start) | collective-permute-done | bytes 65568 | tf_op jit(solution)/shard_map/ppermute | solution.py:18
  10.6 3.9 %collective-permute-start.1 = (bf16[32,2048]{1,0:T(8,128)(2,1)S(1)}, bf16[32,2048]{1,0:T(8,128)(2,1)S(1)}, u32[]{:S(2)}, u32[]{:S(2)}) collective-permute-start(bf16[32,2048]{1,0:T(8,128)(2,1)S(1)} %constant_dynamic-update-slice_fusion.home), channel_id=1, source_target_pairs={{0,2},{1,15},{2,4},{3,1},{4,6},{5,3},{6,8},{7,5},{8,10},{9,7},{10,... | collective-permute-start | bytes 393224 | tf_op jit(solution)/shard_map/ppermute | solution.py:26
  16.1 4.5 %collective-permute-start.4 = (bf16[16,2048]{1,0:T(8,128)(2,1)S(1)}, bf16[16,2048]{1,0:T(8,128)(2,1)S(1)}, u32[]{:S(2)}, u32[]{:S(2)}) collective-permute-start(bf16[16,2048]{1,0:T(8,128)(2,1)S(1)} %copy-done.7), channel_id=1, source_target_pairs={{0,8},{1,9},{2,10},{3,11},{4,12},{5,13},{6,14},{7,15},{8,0},{9,1},... | collective-permute-start | bytes 196616 | tf_op jit(solution)/shard_map/ppermute | solution.py:26
  20.5 5.9 %collective-permute-done.4.four = bf16[16,2048]{1,0:T(8,128)(2,1)S(1)} collective-permute-done((bf16[16,2048]{1,0:T(8,128)(2,1)S(1)}, bf16[16,2048]{1,0:T(8,128)(2,1)S(1)}, u32[]{:S(2)}, u32[]{:S(2)}) %collective-permute-start.4) | collective-permute-done | bytes 65568 | tf_op jit(solution)/shard_map/ppermute | solution.py:26
  33.6 4.0 %all-to-all-start = ((bf16[4,64,512]{2,1,0:T(8,128)(2,1)}), bf16[4,64,512]{2,1,0:T(8,128)(2,1)S(1)}, u32[]{:S(2)}, u32[]{:S(2)}) async-start(bf16[4,64,512]{2,1,0:T(8,128)(2,1)} %bitcast.7), calls=%async_computation | async-start | bytes 524288 | tf_op jit(solution)/shard_map/all_to_all | solution.py:38
  37.6 5.8 %all-to-all-done = bf16[4,64,512]{2,1,0:T(8,128)(2,1)S(1)} async-done(((bf16[4,64,512]{2,1,0:T(8,128)(2,1)}), bf16[4,64,512]{2,1,0:T(8,128)(2,1)S(1)}, u32[]{:S(2)}, u32[]{:S(2)}) %all-to-all-start) | async-done | bytes 262176 | tf_op jit(solution)/shard_map/all_to_all | solution.py:38
  43.5 20.0 %all_to_all.10 = bf16[16,64,512]{2,1,0:T(8,128)(2,1)S(1)} all-to-all(bf16[16,64,512]{2,1,0:T(8,128)(2,1)S(1)} %broadcast_in_dim.85), channel_id=1, replica_groups=mesh['layer'=4,'row'=4,'col'=16] {'layer','row'}, dimensions={0} | all-to-all | bytes 2097152 | tf_op jit(solution)/shard_map/all_to_all | solution.py:38
  63.6 2.9 %collective-permute-start.7 = (bf16[1024,512]{1,0:T(8,128)(2,1)S(1)}, bf16[1024,512]{1,0:T(8,128)(2,1)}, u32[]{:S(2)}, u32[]{:S(2)}) collective-permute-start(bf16[1024,512]{1,0:T(8,128)(2,1)S(1)} %bitcast.97), channel_id=1, source_target_pairs={{0,1},{1,0},{2,3},{3,2},{4,5},{5,4},{6,7},{7,6},{8,9},{9,8},{10,11... | collective-permute-start | bytes 3145736 | tf_op jit(solution)/shard_map/ppermute | solution.py:18
  69.7 2.8 %add_convert_fusion = bf16[1024,1024]{1,0:T(8,128)(2,1)S(1)} fusion(bf16[1024,1024]{1,0:T(8,128)(2,1)S(1)} %select_convert_fusion, bf16[1024,512]{1,0:T(8,128)(2,1)} %collective-permute-done.7, pred[1024]{0:T(1024)(128)(4,1)S(1)} %select_n.165, bf16[576,1024]{1,0:T(8,128)(2,1)} %collective-permute-done.6), kind=kOutput, calls=%fused_computation | convolution fusion | flops 1077936128 | bytes 6292480 | tf_op jit(solution)/shard_map/dot_general | solution.py:50
  82.4 2.7 %collective-permute-start.12 = (bf16[64,1024]{1,0:T(8,128)(2,1)S(1)}, bf16[64,1024]{1,0:T(8,128)(2,1)S(1)}, u32[]{:S(2)}, u32[]{:S(2)}) collective-permute-start(bf16[64,1024]{1,0:T(8,128)(2,1)S(1)} %add_convert_fusion.9), channel_id=1, source_target_pairs={{0,14},{1,15},{2,0},{3,1},{4,2},{5,3},{6,4},{7,5},{8,6},{9,7},{10,... | collective-permute-start | bytes 393224 | tf_op jit(solution)/shard_map/ppermute | solution.py:30
  85.4 2.7 %collective-permute-start.29 = (bf16[64,1024]{1,0:T(8,128)(2,1)S(1)}, bf16[64,1024]{1,0:T(8,128)(2,1)S(1)}, u32[]{:S(2)}, u32[]{:S(2)}) collective-permute-start(bf16[64,1024]{1,0:T(8,128)(2,1)S(1)} %add_convert_fusion.2), channel_id=1, source_target_pairs={{0,14},{1,15},{2,0},{3,1},{4,2},{5,3},{6,4},{7,5},{8,6},{9,7},{10,... | collective-permute-start | bytes 393224 | tf_op jit(solution)/shard_map/ppermute | solution.py:30
  88.3 2.7 %collective-permute-start.13 = (bf16[64,1024]{1,0:T(8,128)(2,1)S(1)}, bf16[64,1024]{1,0:T(8,128)(2,1)S(1)}, u32[]{:S(2)}, u32[]{:S(2)}) collective-permute-start(bf16[64,1024]{1,0:T(8,128)(2,1)S(1)} %add_convert_fusion.8), channel_id=1, source_target_pairs={{0,14},{1,15},{2,0},{3,1},{4,2},{5,3},{6,4},{7,5},{8,6},{9,7},{10,... | collective-permute-start | bytes 393224 | tf_op jit(solution)/shard_map/ppermute | solution.py:30
  91.1 3.0 %collective-permute-done.13 = bf16[64,1024]{1,0:T(8,128)(2,1)S(1)} collective-permute-done((bf16[64,1024]{1,0:T(8,128)(2,1)S(1)}, bf16[64,1024]{1,0:T(8,128)(2,1)S(1)}, u32[]{:S(2)}, u32[]{:S(2)}) %collective-permute-start.13) | collective-permute-done | bytes 131104 | tf_op jit(solution)/shard_map/ppermute | solution.py:30
  94.2 3.3 %collective-permute-start.14 = (bf16[64,1024]{1,0:T(8,128)(2,1)S(1)}, bf16[64,1024]{1,0:T(8,128)(2,1)S(1)}, u32[]{:S(2)}, u32[]{:S(2)}) collective-permute-start(bf16[64,1024]{1,0:T(8,128)(2,1)S(1)} %add_convert_fusion.7), channel_id=1, source_target_pairs={{0,14},{1,15},{2,0},{3,1},{4,2},{5,3},{6,4},{7,5},{8,6},{9,7},{10,... | collective-permute-start | bytes 393224 | tf_op jit(solution)/shard_map/ppermute | solution.py:30
  98.6 2.7 %collective-permute-start.31 = (bf16[64,1024]{1,0:T(8,128)(2,1)}, bf16[64,1024]{1,0:T(8,128)(2,1)S(1)}, u32[]{:S(2)}, u32[]{:S(2)}) collective-permute-start(bf16[64,1024]{1,0:T(8,128)(2,1)} %get-tuple-element.23), channel_id=1, source_target_pairs={{0,14},{1,15},{2,0},{3,1},{4,2},{5,3},{6,4},{7,5},{8,6},{9,7},{10,... | collective-permute-start | bytes 393224 | tf_op jit(solution)/shard_map/ppermute | solution.py:30
  102.1 2.7 %collective-permute-start.16 = (bf16[64,1024]{1,0:T(8,128)(2,1)}, bf16[64,1024]{1,0:T(8,128)(2,1)S(1)}, u32[]{:S(2)}, u32[]{:S(2)}) collective-permute-start(bf16[64,1024]{1,0:T(8,128)(2,1)} %get-tuple-element.25), channel_id=1, source_target_pairs={{0,14},{1,15},{2,0},{3,1},{4,2},{5,3},{6,4},{7,5},{8,6},{9,7},{10,... | collective-permute-start | bytes 393224 | tf_op jit(solution)/shard_map/ppermute | solution.py:30
  109.5 2.8 %collective-permute-start.18 = (bf16[64,1024]{1,0:T(8,128)(2,1)S(1)}, bf16[64,1024]{1,0:T(8,128)(2,1)S(1)}, u32[]{:S(2)}, u32[]{:S(2)}) collective-permute-start(bf16[64,1024]{1,0:T(8,128)(2,1)S(1)} %collective-permute-done.16), channel_id=1, source_target_pairs={{0,14},{1,15},{2,0},{3,1},{4,2},{5,3},{6,4},{7,5},{8,6},{9,7},{10,... | collective-permute-start | bytes 393224 | tf_op jit(solution)/shard_map/ppermute | solution.py:30
  116.4 2.7 %collective-permute-start.20 = (bf16[64,1024]{1,0:T(8,128)(2,1)S(1)}, bf16[64,1024]{1,0:T(8,128)(2,1)S(1)}, u32[]{:S(2)}, u32[]{:S(2)}) collective-permute-start(bf16[64,1024]{1,0:T(8,128)(2,1)S(1)} %collective-permute-done.18), channel_id=1, source_target_pairs={{0,14},{1,15},{2,0},{3,1},{4,2},{5,3},{6,4},{7,5},{8,6},{9,7},{10,... | collective-permute-start | bytes 393224 | tf_op jit(solution)/shard_map/ppermute | solution.py:30
  121.1 3.1 %collective-permute-start.21 = (bf16[64,1024]{1,0:T(8,128)(2,1)S(1)}, bf16[64,1024]{1,0:T(8,128)(2,1)S(1)}, u32[]{:S(2)}, u32[]{:S(2)}) collective-permute-start(bf16[64,1024]{1,0:T(8,128)(2,1)S(1)} %collective-permute-done.20), channel_id=1, source_target_pairs={{0,14},{1,15},{2,0},{3,1},{4,2},{5,3},{6,4},{7,5},{8,6},{9,7},{10,... | collective-permute-start | bytes 393224 | tf_op jit(solution)/shard_map/ppermute | solution.py:30
  126.2 7.4 %collective-permute-start.37 = (bf16[512,1024]{1,0:T(8,128)(2,1)}, bf16[512,1024]{1,0:T(8,128)(2,1)S(1)}, u32[]{:S(2)}, u32[]{:S(2)}) collective-permute-start(bf16[512,1024]{1,0:T(8,128)(2,1)} %bitcast.94), channel_id=1, source_target_pairs={{0,1},{1,0},{2,3},{3,2},{4,5},{5,4},{6,7},{7,6},{8,9},{9,8},{10,11... | collective-permute-start | bytes 3145736 | tf_op jit(solution)/shard_map/ppermute | solution.py:18
  144.4 5.8 %collective-permute-done.38 = bf16[256,512]{1,0:T(8,128)(2,1)S(1)} collective-permute-done((bf16[256,512]{1,0:T(8,128)(2,1)S(1)}, bf16[256,512]{1,0:T(8,128)(2,1)S(1)}, u32[]{:S(2)}, u32[]{:S(2)}) %collective-permute-start.38) | collective-permute-done | bytes 262176 | tf_op jit(solution)/shard_map/ppermute | solution.py:34
  150.2 6.3 %collective-permute-done.39 = bf16[256,512]{1,0:T(8,128)(2,1)S(1)} collective-permute-done((bf16[256,512]{1,0:T(8,128)(2,1)S(1)}, bf16[256,512]{1,0:T(8,128)(2,1)S(1)}, u32[]{:S(2)}, u32[]{:S(2)}) %collective-permute-start.39) | collective-permute-done | bytes 262176 | tf_op jit(solution)/shard_map/ppermute | solution.py:34
  (130 shorter events, 49.8 us)
Async XLA Ops:
  4.5 27.0 %collective-permute-start.6 = (bf16[576,1024]{1,0:T(8,128)(2,1)}, bf16[576,1024]{1,0:T(8,128)(2,1)}, u32[]{:S(2)}, u32[]{:S(2)}) collective-permute-start(bf16[576,1024]{1,0:T(8,128)(2,1)} %pad_maximum_fusion), channel_id=1, source_target_pairs={{0,1},{1,0},{2,3},{3,2},{4,5},{5,4},{6,7},{7,6},{8,9},{9,8},{10,11... | collective-permute-start | bytes 3538952 | tf_op jit(solution)/shard_map/ppermute | solution.py:18
  10.6 15.9 %collective-permute-start.1 = (bf16[32,2048]{1,0:T(8,128)(2,1)S(1)}, bf16[32,2048]{1,0:T(8,128)(2,1)S(1)}, u32[]{:S(2)}, u32[]{:S(2)}) collective-permute-start(bf16[32,2048]{1,0:T(8,128)(2,1)S(1)} %constant_dynamic-update-slice_fusion.home), channel_id=1, source_target_pairs={{0,2},{1,15},{2,4},{3,1},{4,6},{5,3},{6,8},{7,5},{8,10},{9,7},{10,... | collective-permute-start | bytes 393224 | tf_op jit(solution)/shard_map/ppermute | solution.py:26
  14.4 12.0 %collective-permute-start.2 = (bf16[32,2048]{1,0:T(8,128)(2,1)S(1)}, bf16[32,2048]{1,0:T(8,128)(2,1)S(1)}, u32[]{:S(2)}, u32[]{:S(2)}) collective-permute-start(bf16[32,2048]{1,0:T(8,128)(2,1)S(1)} %constant_dynamic-update-slice_fusion.home), channel_id=1, source_target_pairs={{0,4},{1,13},{2,6},{3,15},{4,8},{5,1},{6,10},{7,3},{8,12},{9,5},{1... | collective-permute-start | bytes 393224 | tf_op jit(solution)/shard_map/ppermute | solution.py:26
  15.6 10.9 %collective-permute-start.3 = (bf16[32,2048]{1,0:T(8,128)(2,1)S(1)}, bf16[32,2048]{1,0:T(8,128)(2,1)S(1)}, u32[]{:S(2)}, u32[]{:S(2)}) collective-permute-start(bf16[32,2048]{1,0:T(8,128)(2,1)S(1)} %constant_dynamic-update-slice_fusion.home), channel_id=1, source_target_pairs={{0,6},{1,11},{2,8},{3,13},{4,10},{5,15},{6,12},{7,1},{8,14},{9,3},... | collective-permute-start | bytes 393224 | tf_op jit(solution)/shard_map/ppermute | solution.py:26
  16.1 10.4 %collective-permute-start.4 = (bf16[16,2048]{1,0:T(8,128)(2,1)S(1)}, bf16[16,2048]{1,0:T(8,128)(2,1)S(1)}, u32[]{:S(2)}, u32[]{:S(2)}) collective-permute-start(bf16[16,2048]{1,0:T(8,128)(2,1)S(1)} %copy-done.7), channel_id=1, source_target_pairs={{0,8},{1,9},{2,10},{3,11},{4,12},{5,13},{6,14},{7,15},{8,0},{9,1},... | collective-permute-start | bytes 196616 | tf_op jit(solution)/shard_map/ppermute | solution.py:26
  33.6 9.8 %all-to-all-start = ((bf16[4,64,512]{2,1,0:T(8,128)(2,1)}), bf16[4,64,512]{2,1,0:T(8,128)(2,1)S(1)}, u32[]{:S(2)}, u32[]{:S(2)}) async-start(bf16[4,64,512]{2,1,0:T(8,128)(2,1)} %bitcast.7), calls=%async_computation | async-start | bytes 524288 | tf_op jit(solution)/shard_map/all_to_all | solution.py:38
  85.4 12.1 %collective-permute-start.29 = (bf16[64,1024]{1,0:T(8,128)(2,1)S(1)}, bf16[64,1024]{1,0:T(8,128)(2,1)S(1)}, u32[]{:S(2)}, u32[]{:S(2)}) collective-permute-start(bf16[64,1024]{1,0:T(8,128)(2,1)S(1)} %add_convert_fusion.2), channel_id=1, source_target_pairs={{0,14},{1,15},{2,0},{3,1},{4,2},{5,3},{6,4},{7,5},{8,6},{9,7},{10,... | collective-permute-start | bytes 393224 | tf_op jit(solution)/shard_map/ppermute | solution.py:30
  88.1 13.1 %collective-permute-start.10 = (bf16[64,1024]{1,0:T(8,128)(2,1)S(1)}, bf16[64,1024]{1,0:T(8,128)(2,1)S(1)}, u32[]{:S(2)}, u32[]{:S(2)}) collective-permute-start(bf16[64,1024]{1,0:T(8,128)(2,1)S(1)} %add_convert_fusion.10), channel_id=1, source_target_pairs={{0,2},{1,3},{2,4},{3,5},{4,6},{5,7},{6,8},{7,9},{8,10},{9,11},{10,... | collective-permute-start | bytes 393224 | tf_op jit(solution)/shard_map/ppermute | solution.py:30
  91.1 6.7 %collective-permute-start.26 = (bf16[64,1024]{1,0:T(8,128)(2,1)S(1)}, bf16[64,1024]{1,0:T(8,128)(2,1)S(1)}, u32[]{:S(2)}, u32[]{:S(2)}) collective-permute-start(bf16[64,1024]{1,0:T(8,128)(2,1)S(1)} %add_convert_fusion.4), channel_id=1, source_target_pairs={{0,2},{1,3},{2,4},{3,5},{4,6},{5,7},{6,8},{7,9},{8,10},{9,11},{10,... | collective-permute-start | bytes 393224 | tf_op jit(solution)/shard_map/ppermute | solution.py:30
  94.2 7.1 %collective-permute-start.14 = (bf16[64,1024]{1,0:T(8,128)(2,1)S(1)}, bf16[64,1024]{1,0:T(8,128)(2,1)S(1)}, u32[]{:S(2)}, u32[]{:S(2)}) collective-permute-start(bf16[64,1024]{1,0:T(8,128)(2,1)S(1)} %add_convert_fusion.7), channel_id=1, source_target_pairs={{0,14},{1,15},{2,0},{3,1},{4,2},{5,3},{6,4},{7,5},{8,6},{9,7},{10,... | collective-permute-start | bytes 393224 | tf_op jit(solution)/shard_map/ppermute | solution.py:30
  102.1 6.7 %collective-permute-start.15 = (bf16[64,1024]{1,0:T(8,128)(2,1)}, bf16[64,1024]{1,0:T(8,128)(2,1)S(1)}, u32[]{:S(2)}, u32[]{:S(2)}) collective-permute-start(bf16[64,1024]{1,0:T(8,128)(2,1)} %get-tuple-element.25), channel_id=1, source_target_pairs={{0,2},{1,3},{2,4},{3,5},{4,6},{5,7},{6,8},{7,9},{8,10},{9,11},{10,... | collective-permute-start | bytes 393224 | tf_op jit(solution)/shard_map/ppermute | solution.py:30
  102.1 7.3 %collective-permute-start.16 = (bf16[64,1024]{1,0:T(8,128)(2,1)}, bf16[64,1024]{1,0:T(8,128)(2,1)S(1)}, u32[]{:S(2)}, u32[]{:S(2)}) collective-permute-start(bf16[64,1024]{1,0:T(8,128)(2,1)} %get-tuple-element.25), channel_id=1, source_target_pairs={{0,14},{1,15},{2,0},{3,1},{4,2},{5,3},{6,4},{7,5},{8,6},{9,7},{10,... | collective-permute-start | bytes 393224 | tf_op jit(solution)/shard_map/ppermute | solution.py:30
  104.8 8.1 %collective-permute-start.32 = (bf16[64,1024]{1,0:T(8,128)(2,1)S(1)}, bf16[64,1024]{1,0:T(8,128)(2,1)S(1)}, u32[]{:S(2)}, u32[]{:S(2)}) collective-permute-start(bf16[64,1024]{1,0:T(8,128)(2,1)S(1)} %collective-permute-done.30), channel_id=1, source_target_pairs={{0,2},{1,3},{2,4},{3,5},{4,6},{5,7},{6,8},{7,9},{8,10},{9,11},{10,... | collective-permute-start | bytes 393224 | tf_op jit(solution)/shard_map/ppermute | solution.py:30
  104.8 8.2 %collective-permute-start.33 = (bf16[64,1024]{1,0:T(8,128)(2,1)S(1)}, bf16[64,1024]{1,0:T(8,128)(2,1)S(1)}, u32[]{:S(2)}, u32[]{:S(2)}) collective-permute-start(bf16[64,1024]{1,0:T(8,128)(2,1)S(1)} %collective-permute-done.31), channel_id=1, source_target_pairs={{0,14},{1,15},{2,0},{3,1},{4,2},{5,3},{6,4},{7,5},{8,6},{9,7},{10,... | collective-permute-start | bytes 393224 | tf_op jit(solution)/shard_map/ppermute | solution.py:30
  108.8 6.9 %collective-permute-start.17 = (bf16[64,1024]{1,0:T(8,128)(2,1)S(1)}, bf16[64,1024]{1,0:T(8,128)(2,1)S(1)}, u32[]{:S(2)}, u32[]{:S(2)}) collective-permute-start(bf16[64,1024]{1,0:T(8,128)(2,1)S(1)} %collective-permute-done.15), channel_id=1, source_target_pairs={{0,2},{1,3},{2,4},{3,5},{4,6},{5,7},{6,8},{7,9},{8,10},{9,11},{10,... | collective-permute-start | bytes 393224 | tf_op jit(solution)/shard_map/ppermute | solution.py:30
  109.5 6.9 %collective-permute-start.18 = (bf16[64,1024]{1,0:T(8,128)(2,1)S(1)}, bf16[64,1024]{1,0:T(8,128)(2,1)S(1)}, u32[]{:S(2)}, u32[]{:S(2)}) collective-permute-start(bf16[64,1024]{1,0:T(8,128)(2,1)S(1)} %collective-permute-done.16), channel_id=1, source_target_pairs={{0,14},{1,15},{2,0},{3,1},{4,2},{5,3},{6,4},{7,5},{8,6},{9,7},{10,... | collective-permute-start | bytes 393224 | tf_op jit(solution)/shard_map/ppermute | solution.py:30
  112.9 6.9 %collective-permute-start.34 = (bf16[64,1024]{1,0:T(8,128)(2,1)S(1)}, bf16[64,1024]{1,0:T(8,128)(2,1)S(1)}, u32[]{:S(2)}, u32[]{:S(2)}) collective-permute-start(bf16[64,1024]{1,0:T(8,128)(2,1)S(1)} %collective-permute-done.32), channel_id=1, source_target_pairs={{0,2},{1,3},{2,4},{3,5},{4,6},{5,7},{6,8},{7,9},{8,10},{9,11},{10,... | collective-permute-start | bytes 393224 | tf_op jit(solution)/shard_map/ppermute | solution.py:30
  113.0 11.8 %collective-permute-start.35 = (bf16[64,1024]{1,0:T(8,128)(2,1)S(1)}, bf16[64,1024]{1,0:T(8,128)(2,1)S(1)}, u32[]{:S(2)}, u32[]{:S(2)}) collective-permute-start(bf16[64,1024]{1,0:T(8,128)(2,1)S(1)} %collective-permute-done.33), channel_id=1, source_target_pairs={{0,14},{1,15},{2,0},{3,1},{4,2},{5,3},{6,4},{7,5},{8,6},{9,7},{10,... | collective-permute-start | bytes 393224 | tf_op jit(solution)/shard_map/ppermute | solution.py:30
  115.7 9.1 %collective-permute-start.19 = (bf16[64,1024]{1,0:T(8,128)(2,1)S(1)}, bf16[64,1024]{1,0:T(8,128)(2,1)S(1)}, u32[]{:S(2)}, u32[]{:S(2)}) collective-permute-start(bf16[64,1024]{1,0:T(8,128)(2,1)S(1)} %collective-permute-done.17), channel_id=1, source_target_pairs={{0,2},{1,3},{2,4},{3,5},{4,6},{5,7},{6,8},{7,9},{8,10},{9,11},{10,... | collective-permute-start | bytes 393224 | tf_op jit(solution)/shard_map/ppermute | solution.py:30
  121.1 12.5 %collective-permute-start.21 = (bf16[64,1024]{1,0:T(8,128)(2,1)S(1)}, bf16[64,1024]{1,0:T(8,128)(2,1)S(1)}, u32[]{:S(2)}, u32[]{:S(2)}) collective-permute-start(bf16[64,1024]{1,0:T(8,128)(2,1)S(1)} %collective-permute-done.20), channel_id=1, source_target_pairs={{0,14},{1,15},{2,0},{3,1},{4,2},{5,3},{6,4},{7,5},{8,6},{9,7},{10,... | collective-permute-start | bytes 393224 | tf_op jit(solution)/shard_map/ppermute | solution.py:30
  126.2 9.9 %collective-permute-start.37 = (bf16[512,1024]{1,0:T(8,128)(2,1)}, bf16[512,1024]{1,0:T(8,128)(2,1)S(1)}, u32[]{:S(2)}, u32[]{:S(2)}) collective-permute-start(bf16[512,1024]{1,0:T(8,128)(2,1)} %bitcast.94), channel_id=1, source_target_pairs={{0,1},{1,0},{2,3},{3,2},{4,5},{5,4},{6,7},{7,6},{8,9},{9,8},{10,11... | collective-permute-start | bytes 3145736 | tf_op jit(solution)/shard_map/ppermute | solution.py:18
  141.0 9.1 %collective-permute-start.38 = (bf16[256,512]{1,0:T(8,128)(2,1)S(1)}, bf16[256,512]{1,0:T(8,128)(2,1)S(1)}, u32[]{:S(2)}, u32[]{:S(2)}) collective-permute-start(bf16[256,512]{1,0:T(8,128)(2,1)S(1)} %get-tuple-element.19), channel_id=1, source_target_pairs={{0,32},{16,48},{32,0},{48,16},{1,33},{17,49},{33,1},{49,17},{2,34}... | collective-permute-start | bytes 786440 | tf_op jit(solution)/shard_map/ppermute | solution.py:34
  141.7 14.8 %collective-permute-start.39 = (bf16[256,512]{1,0:T(8,128)(2,1)S(1)}, bf16[256,512]{1,0:T(8,128)(2,1)S(1)}, u32[]{:S(2)}, u32[]{:S(2)}) collective-permute-start(bf16[256,512]{1,0:T(8,128)(2,1)S(1)} %get-tuple-element.20), channel_id=1, source_target_pairs={{0,16},{16,32},{32,48},{48,0},{1,17},{17,33},{33,49},{49,1},{2,18}... | collective-permute-start | bytes 786440 | tf_op jit(solution)/shard_map/ppermute | solution.py:34
  141.8 14.7 %collective-permute-start.40 = (bf16[256,512]{1,0:T(8,128)(2,1)S(1)}, bf16[256,512]{1,0:T(8,128)(2,1)S(1)}, u32[]{:S(2)}, u32[]{:S(2)}) collective-permute-start(bf16[256,512]{1,0:T(8,128)(2,1)S(1)} %get-tuple-element.21), channel_id=1, source_target_pairs={{0,48},{16,0},{32,16},{48,32},{1,49},{17,1},{33,17},{49,33},{2,50}... | collective-permute-start | bytes 786440 | tf_op jit(solution)/shard_map/ppermute | solution.py:34
  (26 other events, 233.2 us)

commit v3 on v2

--- a/solution.py
+++ b/solution.py
@@ -144,10 +144,15 @@
     )
     away = to_core(away)
     others = to_core(jnp.concatenate([one, two, three, four]))
-    others, away, couple_own, rhs_own = lax.optimization_barrier((others, away, couple_own, rhs_own))
-    couple_far, rhs_far = away[:height], away[height:]
+    couple_far = lax.optimization_barrier(
+        lax.dynamic_slice(away, (z >> 3, 0), (height, half))
+    )
+    rhs_far = away[height:]
     rhs = lax.optimization_barrier(
         (jnp.where(first, rhs_own, rhs_far), jnp.where(first, rhs_far, rhs_own))
+    )
+    others, couple_far, rhs, couple_own = lax.optimization_barrier(
+        (others, couple_far, rhs, couple_own)
     )
     masks = lax.dynamic_slice(pattern[0], (2 * z, r * blocks + c * (blocks // 2)), (2, blocks // 2))
     masks = jnp.repeat(masks != 0, half // (blocks // 2), axis=1)

time: 158 us -> 157 us (level)
  local copies, waits for them, and re-layouts: 9.56 us -> 13 us
  waiting for transfers between devices: 36.9 us -> 34.4 us
    dynamic_slice x1 -> x2, local copies, waits for them, and re-layouts: 0.02 us -> 3.44 us  [the longest x1 2.52 us: on_device(): lax.dynamic_slice(away, (z >> 3, 0), (height, half))]
    ppermute x6, waiting for transfers between devices: 6.32 us -> 4.71 us  [to_core(): return lax.ppermute(x, 'col', [(i, i ^ 1) for i in range(2 * NZ)])]
  transfers between devices with their start and end apart: 42 -> 42, of which waited for: 13 -> 14; matrix products, arithmetic and copies ran while one was open for 7% -> 8% of each run, Pallas kernels for 1% -> 1%
where the time goes in v3:
time: 157 us; the launch traced here: 156 us
  starting transfers between devices  73.7 us (47%)
  waiting for transfers between devices  34.4 us (22%)
  blocking collectives  20.4 us (13%)
  local copies, waits for them, and re-layouts  13 us (8%)
  other arithmetic  5.68 us (4%)
  Pallas kernels  5.67 us (4%)
  matrix products  2.55 us (2%)
    ppermute x28, starting transfers between devices, along_z(): lax.ppermute(x, 'col', [(i, (i + 2 * step) % (2 * NZ)) for i in range(2 *...  39.9 us
    all_to_all x1, blocking collectives, exchange(): return lax.all_to_all(x, axes, 0, 0, tiled=True)  20.4 us
    ppermute x6, starting transfers between devices, to_core(): return lax.ppermute(x, 'col', [(i, i ^ 1) for i in range(2 * NZ)])  16.5 us
    ppermute x3, waiting for transfers between devices, along_x(): return lax.ppermute(x, 'row', [(i, (i + step) % NX) for i in range(NX)])  12.2 us
    ppermute x4, starting transfers between devices, twisted(): return lax.ppermute(x, 'col', pairs)  9.97 us
    all_to_all x1, waiting for transfers between devices, exchange(): return lax.all_to_all(x, axes, 0, 0, tiled=True)  6.18 us
    ppermute x4, waiting for transfers between devices, twisted(): return lax.ppermute(x, 'col', pairs)  5.93 us
    pallas_call x3, Pallas kernels, local_call(): pl.pallas_call(kernel, out_shape=shapes, in_specs=[pl.BlockSpec(memory_sp...  5.67 us
  transfers between devices with their start and end apart: 42, of which 14 were waited for; matrix products, arithmetic and copies ran while one was open for 8% of the time, Pallas kernels for 1%

profile of v3, /device:TPU:1, one launch (start us, length us, event | category | flops | bytes accessed | tf_op | source)
XLA Modules:
  0.0 156.4 jit_solution(10906276032675480871)
XLA Ops:
  1.6 2.7 %dynamic-slice_bitcast_fusion = (bf16[512,1024]{1,0:T(8,128)(2,1)}, bf16[512,1024]{1,0:T(8,128)(2,1)S(1)}) fusion(bf16[1,512,2048]{2,1,0:T(8,128)(2,1)} %param.10, s32[]{:T(128)S(6)} %select_n.157, s32[]{:T(128)S(6)} %select_n.154), kind=kLoop, calls=%fused_computation.3 | loop fusion | bytes 4194312 | tf_op jit(solution)/shard_map/dynamic_slice | solution.py:137
  5.4 3.2 %collective-permute-start.6 = (bf16[576,1024]{1,0:T(8,128)(2,1)}, bf16[576,1024]{1,0:T(8,128)(2,1)}, u32[]{:S(2)}, u32[]{:S(2)}) collective-permute-start(bf16[576,1024]{1,0:T(8,128)(2,1)} %pad_maximum_fusion), channel_id=1, source_target_pairs={{0,1},{1,0},{2,3},{3,2},{4,5},{5,4},{6,7},{7,6},{8,9},{9,8},{10,11... | collective-permute-start | bytes 3538952 | tf_op jit(solution)/shard_map/ppermute | solution.py:18
  8.7 2.7 %collective-permute-done = bf16[16,2048]{1,0:T(8,128)(2,1)S(1)} collective-permute-done((bf16[16,2048]{1,0:T(8,128)(2,1)S(1)}, bf16[16,2048]{1,0:T(8,128)(2,1)S(1)}, u32[]{:S(2)}, u32[]{:S(2)}) %collective-permute-start) | collective-permute-done | bytes 65568 | tf_op jit(solution)/shard_map/ppermute | solution.py:18
  11.4 3.9 %collective-permute-start.1 = (bf16[32,2048]{1,0:T(8,128)(2,1)S(1)}, bf16[32,2048]{1,0:T(8,128)(2,1)S(1)}, u32[]{:S(2)}, u32[]{:S(2)}) collective-permute-start(bf16[32,2048]{1,0:T(8,128)(2,1)S(1)} %constant_dynamic-update-slice_fusion.home), channel_id=1, source_target_pairs={{0,2},{1,15},{2,4},{3,1},{4,6},{5,3},{6,8},{7,5},{8,10},{9,7},{10,... | collective-permute-start | bytes 393224 | tf_op jit(solution)/shard_map/ppermute | solution.py:26
  16.9 4.5 %collective-permute-start.4 = (bf16[16,2048]{1,0:T(8,128)(2,1)S(1)}, bf16[16,2048]{1,0:T(8,128)(2,1)S(1)}, u32[]{:S(2)}, u32[]{:S(2)}) collective-permute-start(bf16[16,2048]{1,0:T(8,128)(2,1)S(1)} %copy-done.8), channel_id=1, source_target_pairs={{0,8},{1,9},{2,10},{3,11},{4,12},{5,13},{6,14},{7,15},{8,0},{9,1},... | collective-permute-start | bytes 196616 | tf_op jit(solution)/shard_map/ppermute | solution.py:26
  21.4 5.9 %collective-permute-done.4.four = bf16[16,2048]{1,0:T(8,128)(2,1)S(1)} collective-permute-done((bf16[16,2048]{1,0:T(8,128)(2,1)S(1)}, bf16[16,2048]{1,0:T(8,128)(2,1)S(1)}, u32[]{:S(2)}, u32[]{:S(2)}) %collective-permute-start.4) | collective-permute-done | bytes 65568 | tf_op jit(solution)/shard_map/ppermute | solution.py:26
  27.4 2.7 %collective-permute-start.5 = (bf16[112,2048]{1,0:T(8,128)(2,1)S(1)}, bf16[112,2048]{1,0:T(8,128)(2,1)S(1)}, u32[]{:S(2)}, u32[]{:S(2)}) collective-permute-start(bf16[112,2048]{1,0:T(8,128)(2,1)S(1)} %pad_maximum_fusion.1), channel_id=1, source_target_pairs={{0,1},{1,0},{2,3},{3,2},{4,5},{5,4},{6,7},{7,6},{8,9},{9,8},{10,11... | collective-permute-start | bytes 1376264 | tf_op jit(solution)/shard_map/ppermute | solution.py:18
  35.6 4.1 %all-to-all-start = ((bf16[4,64,512]{2,1,0:T(8,128)(2,1)}), bf16[4,64,512]{2,1,0:T(8,128)(2,1)S(1)}, u32[]{:S(2)}, u32[]{:S(2)}) async-start(bf16[4,64,512]{2,1,0:T(8,128)(2,1)} %bitcast.7), calls=%async_computation | async-start | bytes 524288 | tf_op jit(solution)/shard_map/all_to_all | solution.py:38
  39.8 6.2 %all-to-all-done = bf16[4,64,512]{2,1,0:T(8,128)(2,1)S(1)} async-done(((bf16[4,64,512]{2,1,0:T(8,128)(2,1)}), bf16[4,64,512]{2,1,0:T(8,128)(2,1)S(1)}, u32[]{:S(2)}, u32[]{:S(2)}) %all-to-all-start) | async-done | bytes 262176 | tf_op jit(solution)/shard_map/all_to_all | solution.py:38
  46.1 20.4 %all_to_all.10 = bf16[16,64,512]{2,1,0:T(8,128)(2,1)S(1)} all-to-all(bf16[16,64,512]{2,1,0:T(8,128)(2,1)S(1)} %broadcast_in_dim.85), channel_id=1, replica_groups=mesh['layer'=4,'row'=4,'col'=16] {'layer','row'}, dimensions={0} | all-to-all | bytes 2097152 | tf_op jit(solution)/shard_map/all_to_all | solution.py:38
  84.8 2.7 %collective-permute-start.29 = (bf16[64,1024]{1,0:T(8,128)(2,1)S(1)}, bf16[64,1024]{1,0:T(8,128)(2,1)S(1)}, u32[]{:S(2)}, u32[]{:S(2)}) collective-permute-start(bf16[64,1024]{1,0:T(8,128)(2,1)S(1)} %add_convert_fusion.2), channel_id=1, source_target_pairs={{0,14},{1,15},{2,0},{3,1},{4,2},{5,3},{6,4},{7,5},{8,6},{9,7},{10,... | collective-permute-start | bytes 393224 | tf_op jit(solution)/shard_map/ppermute | solution.py:30
  87.8 2.7 %collective-permute-start.13 = (bf16[64,1024]{1,0:T(8,128)(2,1)S(1)}, bf16[64,1024]{1,0:T(8,128)(2,1)S(1)}, u32[]{:S(2)}, u32[]{:S(2)}) collective-permute-start(bf16[64,1024]{1,0:T(8,128)(2,1)S(1)} %add_convert_fusion.8), channel_id=1, source_target_pairs={{0,14},{1,15},{2,0},{3,1},{4,2},{5,3},{6,4},{7,5},{8,6},{9,7},{10,... | collective-permute-start | bytes 393224 | tf_op jit(solution)/shard_map/ppermute | solution.py:30
  90.7 2.9 %collective-permute-done.13 = bf16[64,1024]{1,0:T(8,128)(2,1)S(1)} collective-permute-done((bf16[64,1024]{1,0:T(8,128)(2,1)S(1)}, bf16[64,1024]{1,0:T(8,128)(2,1)S(1)}, u32[]{:S(2)}, u32[]{:S(2)}) %collective-permute-start.13) | collective-permute-done | bytes 131104 | tf_op jit(solution)/shard_map/ppermute | solution.py:30
  93.6 3.5 %collective-permute-start.14 = (bf16[64,1024]{1,0:T(8,128)(2,1)S(1)}, bf16[64,1024]{1,0:T(8,128)(2,1)S(1)}, u32[]{:S(2)}, u32[]{:S(2)}) collective-permute-start(bf16[64,1024]{1,0:T(8,128)(2,1)S(1)} %add_convert_fusion.7), channel_id=1, source_target_pairs={{0,14},{1,15},{2,0},{3,1},{4,2},{5,3},{6,4},{7,5},{8,6},{9,7},{10,... | collective-permute-start | bytes 393224 | tf_op jit(solution)/shard_map/ppermute | solution.py:30
  98.0 2.7 %collective-permute-start.31 = (bf16[64,1024]{1,0:T(8,128)(2,1)}, bf16[64,1024]{1,0:T(8,128)(2,1)S(1)}, u32[]{:S(2)}, u32[]{:S(2)}) collective-permute-start(bf16[64,1024]{1,0:T(8,128)(2,1)} %get-tuple-element.25), channel_id=1, source_target_pairs={{0,14},{1,15},{2,0},{3,1},{4,2},{5,3},{6,4},{7,5},{8,6},{9,7},{10,... | collective-permute-start | bytes 393224 | tf_op jit(solution)/shard_map/ppermute | solution.py:30
  101.5 2.7 %collective-permute-start.16 = (bf16[64,1024]{1,0:T(8,128)(2,1)}, bf16[64,1024]{1,0:T(8,128)(2,1)S(1)}, u32[]{:S(2)}, u32[]{:S(2)}) collective-permute-start(bf16[64,1024]{1,0:T(8,128)(2,1)} %get-tuple-element.27), channel_id=1, source_target_pairs={{0,14},{1,15},{2,0},{3,1},{4,2},{5,3},{6,4},{7,5},{8,6},{9,7},{10,... | collective-permute-start | bytes 393224 | tf_op jit(solution)/shard_map/ppermute | solution.py:30
  104.3 3.2 %collective-permute-start.33 = (bf16[64,1024]{1,0:T(8,128)(2,1)S(1)}, bf16[64,1024]{1,0:T(8,128)(2,1)S(1)}, u32[]{:S(2)}, u32[]{:S(2)}) collective-permute-start(bf16[64,1024]{1,0:T(8,128)(2,1)S(1)} %collective-permute-done.31), channel_id=1, source_target_pairs={{0,14},{1,15},{2,0},{3,1},{4,2},{5,3},{6,4},{7,5},{8,6},{9,7},{10,... | collective-permute-start | bytes 393224 | tf_op jit(solution)/shard_map/ppermute | solution.py:30
  108.4 2.8 %collective-permute-start.18 = (bf16[64,1024]{1,0:T(8,128)(2,1)S(1)}, bf16[64,1024]{1,0:T(8,128)(2,1)S(1)}, u32[]{:S(2)}, u32[]{:S(2)}) collective-permute-start(bf16[64,1024]{1,0:T(8,128)(2,1)S(1)} %collective-permute-done.16), channel_id=1, source_target_pairs={{0,14},{1,15},{2,0},{3,1},{4,2},{5,3},{6,4},{7,5},{8,6},{9,7},{10,... | collective-permute-start | bytes 393224 | tf_op jit(solution)/shard_map/ppermute | solution.py:30
  112.0 2.7 %collective-permute-start.35 = (bf16[64,1024]{1,0:T(8,128)(2,1)S(1)}, bf16[64,1024]{1,0:T(8,128)(2,1)S(1)}, u32[]{:S(2)}, u32[]{:S(2)}) collective-permute-start(bf16[64,1024]{1,0:T(8,128)(2,1)S(1)} %collective-permute-done.33), channel_id=1, source_target_pairs={{0,14},{1,15},{2,0},{3,1},{4,2},{5,3},{6,4},{7,5},{8,6},{9,7},{10,... | collective-permute-start | bytes 393224 | tf_op jit(solution)/shard_map/ppermute | solution.py:30
  115.4 2.7 %collective-permute-start.20 = (bf16[64,1024]{1,0:T(8,128)(2,1)S(1)}, bf16[64,1024]{1,0:T(8,128)(2,1)S(1)}, u32[]{:S(2)}, u32[]{:S(2)}) collective-permute-start(bf16[64,1024]{1,0:T(8,128)(2,1)S(1)} %collective-permute-done.18), channel_id=1, source_target_pairs={{0,14},{1,15},{2,0},{3,1},{4,2},{5,3},{6,4},{7,5},{8,6},{9,7},{10,... | collective-permute-start | bytes 393224 | tf_op jit(solution)/shard_map/ppermute | solution.py:30
  120.0 3.1 %collective-permute-start.21 = (bf16[64,1024]{1,0:T(8,128)(2,1)S(1)}, bf16[64,1024]{1,0:T(8,128)(2,1)S(1)}, u32[]{:S(2)}, u32[]{:S(2)}) collective-permute-start(bf16[64,1024]{1,0:T(8,128)(2,1)S(1)} %collective-permute-done.20), channel_id=1, source_target_pairs={{0,14},{1,15},{2,0},{3,1},{4,2},{5,3},{6,4},{7,5},{8,6},{9,7},{10,... | collective-permute-start | bytes 393224 | tf_op jit(solution)/shard_map/ppermute | solution.py:30
  125.2 7.5 %collective-permute-start.37 = (bf16[512,1024]{1,0:T(8,128)(2,1)}, bf16[512,1024]{1,0:T(8,128)(2,1)S(1)}, u32[]{:S(2)}, u32[]{:S(2)}) collective-permute-start(bf16[512,1024]{1,0:T(8,128)(2,1)} %bitcast.96), channel_id=1, source_target_pairs={{0,1},{1,0},{2,3},{3,2},{4,5},{5,4},{6,7},{7,6},{8,9},{9,8},{10,11... | collective-permute-start | bytes 3145736 | tf_op jit(solution)/shard_map/ppermute | solution.py:18
  143.3 5.9 %collective-permute-done.38 = bf16[256,512]{1,0:T(8,128)(2,1)S(1)} collective-permute-done((bf16[256,512]{1,0:T(8,128)(2,1)S(1)}, bf16[256,512]{1,0:T(8,128)(2,1)S(1)}, u32[]{:S(2)}, u32[]{:S(2)}) %collective-permute-start.38) | collective-permute-done | bytes 262176 | tf_op jit(solution)/shard_map/ppermute | solution.py:34
  149.2 6.3 %collective-permute-done.39 = bf16[256,512]{1,0:T(8,128)(2,1)S(1)} collective-permute-done((bf16[256,512]{1,0:T(8,128)(2,1)S(1)}, bf16[256,512]{1,0:T(8,128)(2,1)S(1)}, u32[]{:S(2)}, u32[]{:S(2)}) %collective-permute-start.39) | collective-permute-done | bytes 262176 | tf_op jit(solution)/shard_map/ppermute | solution.py:34
  (133 shorter events, 47.7 us)
Async XLA Ops:
  5.4 24.7 %collective-permute-start.6 = (bf16[576,1024]{1,0:T(8,128)(2,1)}, bf16[576,1024]{1,0:T(8,128)(2,1)}, u32[]{:S(2)}, u32[]{:S(2)}) collective-permute-start(bf16[576,1024]{1,0:T(8,128)(2,1)} %pad_maximum_fusion), channel_id=1, source_target_pairs={{0,1},{1,0},{2,3},{3,2},{4,5},{5,4},{6,7},{7,6},{8,9},{9,8},{10,11... | collective-permute-start | bytes 3538952 | tf_op jit(solution)/shard_map/ppermute | solution.py:18
  11.4 15.9 %collective-permute-start.1 = (bf16[32,2048]{1,0:T(8,128)(2,1)S(1)}, bf16[32,2048]{1,0:T(8,128)(2,1)S(1)}, u32[]{:S(2)}, u32[]{:S(2)}) collective-permute-start(bf16[32,2048]{1,0:T(8,128)(2,1)S(1)} %constant_dynamic-update-slice_fusion.home), channel_id=1, source_target_pairs={{0,2},{1,15},{2,4},{3,1},{4,6},{5,3},{6,8},{7,5},{8,10},{9,7},{10,... | collective-permute-start | bytes 393224 | tf_op jit(solution)/shard_map/ppermute | solution.py:26
  15.3 12.0 %collective-permute-start.2 = (bf16[32,2048]{1,0:T(8,128)(2,1)S(1)}, bf16[32,2048]{1,0:T(8,128)(2,1)S(1)}, u32[]{:S(2)}, u32[]{:S(2)}) collective-permute-start(bf16[32,2048]{1,0:T(8,128)(2,1)S(1)} %constant_dynamic-update-slice_fusion.home), channel_id=1, source_target_pairs={{0,4},{1,13},{2,6},{3,15},{4,8},{5,1},{6,10},{7,3},{8,12},{9,5},{1... | collective-permute-start | bytes 393224 | tf_op jit(solution)/shard_map/ppermute | solution.py:26
  16.4 10.9 %collective-permute-start.3 = (bf16[32,2048]{1,0:T(8,128)(2,1)S(1)}, bf16[32,2048]{1,0:T(8,128)(2,1)S(1)}, u32[]{:S(2)}, u32[]{:S(2)}) collective-permute-start(bf16[32,2048]{1,0:T(8,128)(2,1)S(1)} %constant_dynamic-update-slice_fusion.home), channel_id=1, source_target_pairs={{0,6},{1,11},{2,8},{3,13},{4,10},{5,15},{6,12},{7,1},{8,14},{9,3},... | collective-permute-start | bytes 393224 | tf_op jit(solution)/shard_map/ppermute | solution.py:26
  16.9 10.4 %collective-permute-start.4 = (bf16[16,2048]{1,0:T(8,128)(2,1)S(1)}, bf16[16,2048]{1,0:T(8,128)(2,1)S(1)}, u32[]{:S(2)}, u32[]{:S(2)}) collective-permute-start(bf16[16,2048]{1,0:T(8,128)(2,1)S(1)} %copy-done.8), channel_id=1, source_target_pairs={{0,8},{1,9},{2,10},{3,11},{4,12},{5,13},{6,14},{7,15},{8,0},{9,1},... | collective-permute-start | bytes 196616 | tf_op jit(solution)/shard_map/ppermute | solution.py:26
  35.6 10.3 %all-to-all-start = ((bf16[4,64,512]{2,1,0:T(8,128)(2,1)}), bf16[4,64,512]{2,1,0:T(8,128)(2,1)S(1)}, u32[]{:S(2)}, u32[]{:S(2)}) async-start(bf16[4,64,512]{2,1,0:T(8,128)(2,1)} %bitcast.7), calls=%async_computation | async-start | bytes 524288 | tf_op jit(solution)/shard_map/all_to_all | solution.py:38
  84.8 12.3 %collective-permute-start.29 = (bf16[64,1024]{1,0:T(8,128)(2,1)S(1)}, bf16[64,1024]{1,0:T(8,128)(2,1)S(1)}, u32[]{:S(2)}, u32[]{:S(2)}) collective-permute-start(bf16[64,1024]{1,0:T(8,128)(2,1)S(1)} %add_convert_fusion.2), channel_id=1, source_target_pairs={{0,14},{1,15},{2,0},{3,1},{4,2},{5,3},{6,4},{7,5},{8,6},{9,7},{10,... | collective-permute-start | bytes 393224 | tf_op jit(solution)/shard_map/ppermute | solution.py:30
  87.6 13.1 %collective-permute-start.10 = (bf16[64,1024]{1,0:T(8,128)(2,1)S(1)}, bf16[64,1024]{1,0:T(8,128)(2,1)S(1)}, u32[]{:S(2)}, u32[]{:S(2)}) collective-permute-start(bf16[64,1024]{1,0:T(8,128)(2,1)S(1)} %add_convert_fusion.10), channel_id=1, source_target_pairs={{0,2},{1,3},{2,4},{3,5},{4,6},{5,7},{6,8},{7,9},{8,10},{9,11},{10,... | collective-permute-start | bytes 393224 | tf_op jit(solution)/shard_map/ppermute | solution.py:30
  90.6 6.5 %collective-permute-start.26 = (bf16[64,1024]{1,0:T(8,128)(2,1)S(1)}, bf16[64,1024]{1,0:T(8,128)(2,1)S(1)}, u32[]{:S(2)}, u32[]{:S(2)}) collective-permute-start(bf16[64,1024]{1,0:T(8,128)(2,1)S(1)} %add_convert_fusion.4), channel_id=1, source_target_pairs={{0,2},{1,3},{2,4},{3,5},{4,6},{5,7},{6,8},{7,9},{8,10},{9,11},{10,... | collective-permute-start | bytes 393224 | tf_op jit(solution)/shard_map/ppermute | solution.py:30
  93.6 7.0 %collective-permute-start.14 = (bf16[64,1024]{1,0:T(8,128)(2,1)S(1)}, bf16[64,1024]{1,0:T(8,128)(2,1)S(1)}, u32[]{:S(2)}, u32[]{:S(2)}) collective-permute-start(bf16[64,1024]{1,0:T(8,128)(2,1)S(1)} %add_convert_fusion.7), channel_id=1, source_target_pairs={{0,14},{1,15},{2,0},{3,1},{4,2},{5,3},{6,4},{7,5},{8,6},{9,7},{10,... | collective-permute-start | bytes 393224 | tf_op jit(solution)/shard_map/ppermute | solution.py:30
  98.0 6.3 %collective-permute-start.31 = (bf16[64,1024]{1,0:T(8,128)(2,1)}, bf16[64,1024]{1,0:T(8,128)(2,1)S(1)}, u32[]{:S(2)}, u32[]{:S(2)}) collective-permute-start(bf16[64,1024]{1,0:T(8,128)(2,1)} %get-tuple-element.25), channel_id=1, source_target_pairs={{0,14},{1,15},{2,0},{3,1},{4,2},{5,3},{6,4},{7,5},{8,6},{9,7},{10,... | collective-permute-start | bytes 393224 | tf_op jit(solution)/shard_map/ppermute | solution.py:30
  101.5 6.9 %collective-permute-start.16 = (bf16[64,1024]{1,0:T(8,128)(2,1)}, bf16[64,1024]{1,0:T(8,128)(2,1)S(1)}, u32[]{:S(2)}, u32[]{:S(2)}) collective-permute-start(bf16[64,1024]{1,0:T(8,128)(2,1)} %get-tuple-element.27), channel_id=1, source_target_pairs={{0,14},{1,15},{2,0},{3,1},{4,2},{5,3},{6,4},{7,5},{8,6},{9,7},{10,... | collective-permute-start | bytes 393224 | tf_op jit(solution)/shard_map/ppermute | solution.py:30
  104.2 7.7 %collective-permute-start.32 = (bf16[64,1024]{1,0:T(8,128)(2,1)S(1)}, bf16[64,1024]{1,0:T(8,128)(2,1)S(1)}, u32[]{:S(2)}, u32[]{:S(2)}) collective-permute-start(bf16[64,1024]{1,0:T(8,128)(2,1)S(1)} %collective-permute-done.30), channel_id=1, source_target_pairs={{0,2},{1,3},{2,4},{3,5},{4,6},{5,7},{6,8},{7,9},{8,10},{9,11},{10,... | collective-permute-start | bytes 393224 | tf_op jit(solution)/shard_map/ppermute | solution.py:30
  104.3 7.7 %collective-permute-start.33 = (bf16[64,1024]{1,0:T(8,128)(2,1)S(1)}, bf16[64,1024]{1,0:T(8,128)(2,1)S(1)}, u32[]{:S(2)}, u32[]{:S(2)}) collective-permute-start(bf16[64,1024]{1,0:T(8,128)(2,1)S(1)} %collective-permute-done.31), channel_id=1, source_target_pairs={{0,14},{1,15},{2,0},{3,1},{4,2},{5,3},{6,4},{7,5},{8,6},{9,7},{10,... | collective-permute-start | bytes 393224 | tf_op jit(solution)/shard_map/ppermute | solution.py:30
  107.8 6.9 %collective-permute-start.17 = (bf16[64,1024]{1,0:T(8,128)(2,1)S(1)}, bf16[64,1024]{1,0:T(8,128)(2,1)S(1)}, u32[]{:S(2)}, u32[]{:S(2)}) collective-permute-start(bf16[64,1024]{1,0:T(8,128)(2,1)S(1)} %collective-permute-done.15), channel_id=1, source_target_pairs={{0,2},{1,3},{2,4},{3,5},{4,6},{5,7},{6,8},{7,9},{8,10},{9,11},{10,... | collective-permute-start | bytes 393224 | tf_op jit(solution)/shard_map/ppermute | solution.py:30
  108.4 6.9 %collective-permute-start.18 = (bf16[64,1024]{1,0:T(8,128)(2,1)S(1)}, bf16[64,1024]{1,0:T(8,128)(2,1)S(1)}, u32[]{:S(2)}, u32[]{:S(2)}) collective-permute-start(bf16[64,1024]{1,0:T(8,128)(2,1)S(1)} %collective-permute-done.16), channel_id=1, source_target_pairs={{0,14},{1,15},{2,0},{3,1},{4,2},{5,3},{6,4},{7,5},{8,6},{9,7},{10,... | collective-permute-start | bytes 393224 | tf_op jit(solution)/shard_map/ppermute | solution.py:30
  111.9 6.9 %collective-permute-start.34 = (bf16[64,1024]{1,0:T(8,128)(2,1)S(1)}, bf16[64,1024]{1,0:T(8,128)(2,1)S(1)}, u32[]{:S(2)}, u32[]{:S(2)}) collective-permute-start(bf16[64,1024]{1,0:T(8,128)(2,1)S(1)} %collective-permute-done.32), channel_id=1, source_target_pairs={{0,2},{1,3},{2,4},{3,5},{4,6},{5,7},{6,8},{7,9},{8,10},{9,11},{10,... | collective-permute-start | bytes 393224 | tf_op jit(solution)/shard_map/ppermute | solution.py:30
  112.0 11.8 %collective-permute-start.35 = (bf16[64,1024]{1,0:T(8,128)(2,1)S(1)}, bf16[64,1024]{1,0:T(8,128)(2,1)S(1)}, u32[]{:S(2)}, u32[]{:S(2)}) collective-permute-start(bf16[64,1024]{1,0:T(8,128)(2,1)S(1)} %collective-permute-done.33), channel_id=1, source_target_pairs={{0,14},{1,15},{2,0},{3,1},{4,2},{5,3},{6,4},{7,5},{8,6},{9,7},{10,... | collective-permute-start | bytes 393224 | tf_op jit(solution)/shard_map/ppermute | solution.py:30
  114.7 9.1 %collective-permute-start.19 = (bf16[64,1024]{1,0:T(8,128)(2,1)S(1)}, bf16[64,1024]{1,0:T(8,128)(2,1)S(1)}, u32[]{:S(2)}, u32[]{:S(2)}) collective-permute-start(bf16[64,1024]{1,0:T(8,128)(2,1)S(1)} %collective-permute-done.17), channel_id=1, source_target_pairs={{0,2},{1,3},{2,4},{3,5},{4,6},{5,7},{6,8},{7,9},{8,10},{9,11},{10,... | collective-permute-start | bytes 393224 | tf_op jit(solution)/shard_map/ppermute | solution.py:30
  120.0 12.7 %collective-permute-start.21 = (bf16[64,1024]{1,0:T(8,128)(2,1)S(1)}, bf16[64,1024]{1,0:T(8,128)(2,1)S(1)}, u32[]{:S(2)}, u32[]{:S(2)}) collective-permute-start(bf16[64,1024]{1,0:T(8,128)(2,1)S(1)} %collective-permute-done.20), channel_id=1, source_target_pairs={{0,14},{1,15},{2,0},{3,1},{4,2},{5,3},{6,4},{7,5},{8,6},{9,7},{10,... | collective-permute-start | bytes 393224 | tf_op jit(solution)/shard_map/ppermute | solution.py:30
  125.2 10.0 %collective-permute-start.37 = (bf16[512,1024]{1,0:T(8,128)(2,1)}, bf16[512,1024]{1,0:T(8,128)(2,1)S(1)}, u32[]{:S(2)}, u32[]{:S(2)}) collective-permute-start(bf16[512,1024]{1,0:T(8,128)(2,1)} %bitcast.96), channel_id=1, source_target_pairs={{0,1},{1,0},{2,3},{3,2},{4,5},{5,4},{6,7},{7,6},{8,9},{9,8},{10,11... | collective-permute-start | bytes 3145736 | tf_op jit(solution)/shard_map/ppermute | solution.py:18
  140.1 9.1 %collective-permute-start.38 = (bf16[256,512]{1,0:T(8,128)(2,1)S(1)}, bf16[256,512]{1,0:T(8,128)(2,1)S(1)}, u32[]{:S(2)}, u32[]{:S(2)}) collective-permute-start(bf16[256,512]{1,0:T(8,128)(2,1)S(1)} %get-tuple-element.21), channel_id=1, source_target_pairs={{0,32},{16,48},{32,0},{48,16},{1,33},{17,49},{33,1},{49,17},{2,34}... | collective-permute-start | bytes 786440 | tf_op jit(solution)/shard_map/ppermute | solution.py:34
  140.7 14.9 %collective-permute-start.39 = (bf16[256,512]{1,0:T(8,128)(2,1)S(1)}, bf16[256,512]{1,0:T(8,128)(2,1)S(1)}, u32[]{:S(2)}, u32[]{:S(2)}) collective-permute-start(bf16[256,512]{1,0:T(8,128)(2,1)S(1)} %get-tuple-element.22), channel_id=1, source_target_pairs={{0,16},{16,32},{32,48},{48,0},{1,17},{17,33},{33,49},{49,1},{2,18}... | collective-permute-start | bytes 786440 | tf_op jit(solution)/shard_map/ppermute | solution.py:34
  140.9 14.6 %collective-permute-start.40 = (bf16[256,512]{1,0:T(8,128)(2,1)S(1)}, bf16[256,512]{1,0:T(8,128)(2,1)S(1)}, u32[]{:S(2)}, u32[]{:S(2)}) collective-permute-start(bf16[256,512]{1,0:T(8,128)(2,1)S(1)} %get-tuple-element.23), channel_id=1, source_target_pairs={{0,48},{16,0},{32,16},{48,32},{1,49},{17,1},{33,17},{49,33},{2,50}... | collective-permute-start | bytes 786440 | tf_op jit(solution)/shard_map/ppermute | solution.py:34
  (27 other events, 258.2 us)
